TPU v7x, 1024 devices: a whole 4x8x16 slice. The times are simulated.
1024 devices in a mesh: latent: 64 (over x_lo, z, core), blk: 16 (over y, x_hi).
Axes of the slice: x: 4 (x_hi: 2, x_lo: 2; x = x_hi * 2 + x_lo), y: 8, z: 16, core: 2. Of those that a mesh axis runs over, the one named last changes fastest.
Arguments:
- activations: bfloat16 [131072, 8192], P(('latent', 'blk')), may hold values from -90 to 90
- block_ids: int32 [131072, 1], P(('latent', 'blk')), may hold values from 0 to 63; in each aligned block of 128 rows (0 to 127, 128 to 255, ...) at most 2 rows name the same one
- enc_weight: bfloat16 [64, 8192, 128], P('latent'), may hold values from -0.0625 to 0.0625
- enc_bias: float32 [64, 128], P('latent'), may hold values from -3 to 3
- dec_weight: bfloat16 [64, 128, 8192], P('latent'), may hold values from -0.5 to 0.5
- dec_bias: float32 [8192], replicated, may hold values from -5 to 5
Outputs:
- recon_loss: float32 [], replicated
- latent_codes: bfloat16 [131072, 128], P(('latent', 'blk'))
- dec_weight_grad: float32 [64, 128, 8192], P('latent', None, 'blk')
Inputs may be any that keep to these rules, and one draw needn't show every extreme that they name: `block_ids`: among the rows of one device, every block number is named by exactly 2 rows.
All inputs are finite; a program needn't handle non-finite values.
Results may differ from a plain program's by a relative error of at most 0.0095.
Values may be sent and summed in bfloat16 or wider, within the bound.
No kernel may reach another device: no remote copies, remote signals or barrier semaphores. Data moves between devices by JAX's collectives and lax.ppermute only.
A program may use at most 64 MiB of HBM per device.

v0:
```python
import jax
import jax.numpy as jnp
from jax import lax
from jax.sharding import PartitionSpec as P


def local(activations, block_ids, enc_weight, enc_bias, dec_weight, dec_bias):
    groups = lax.axis_size("latent")
    replicas = lax.axis_size("blk")
    tok_rows = activations.shape[0]
    features = activations.shape[1]
    per_owner = tok_rows // groups
    block_of = block_ids[:, 0]
    matches = (block_of[:, None] == block_of[None, :]).astype(jnp.int32)
    earlier = jnp.sum(jnp.tril(matches, -1), axis=1)
    placed = block_of * per_owner + earlier
    source_row = (
        jnp.zeros((tok_rows,), jnp.int32).at[placed].set(jnp.arange(tok_rows, dtype=jnp.int32))
    )
    outgoing = activations[source_row]
    rows_block = tok_rows * replicas
    contract = (((0,), (0,)), ((), ()))
    incoming = lax.all_to_all(outgoing, "latent", split_axis=0, concat_axis=0, tiled=True)
    centered = (incoming.astype(jnp.float32) - dec_bias).astype(jnp.bfloat16)
    pre_codes = jnp.dot(centered, enc_weight[0], preferred_element_type=jnp.float32) + enc_bias[0]
    codes = jnp.maximum(pre_codes, 0.0).astype(jnp.bfloat16)
    error_rows = (
        jnp.dot(codes, dec_weight[0], preferred_element_type=jnp.float32)
        + dec_bias
        - incoming.astype(jnp.float32)
    )
    squares = jnp.sum(error_rows * error_rows)
    partial_grad = lax.dot_general(
        codes, error_rows.astype(jnp.bfloat16), contract, preferred_element_type=jnp.float32
    )
    summed = lax.psum_scatter(
        partial_grad.astype(jnp.bfloat16), "blk", scatter_dimension=1, tiled=True
    ).astype(jnp.float32)
    returned = lax.all_to_all(codes, "latent", split_axis=0, concat_axis=0, tiled=True)
    token_codes = returned[placed]
    gradient = summed / rows_block
    summed_loss = lax.psum(squares, ("latent", "blk"))
    loss_value = summed_loss / (tok_rows * groups * replicas * features)
    return (loss_value, token_codes, gradient[None])


def solution(mesh):
    placed = (
        P(("latent", "blk"), None),
        P(("latent", "blk"), None),
        P("latent", None, None),
        P("latent", None),
        P("latent", None, None),
        P(),
    )
    return jax.shard_map(
        local,
        mesh=mesh,
        in_specs=placed,
        out_specs=(P(), P(("latent", "blk"), None), P("latent", None, "blk")),
        check_vma=False,
    )
```

profile of v0, /device:TPU:1, one launch (start us, length us, event | category | flops | bytes accessed | tf_op | source)
XLA Modules:
  0.0 389.7 jit_solution(7547305977954152415)
XLA Ops:
  7.2 0.0 copy-start
  7.2 0.0 reduce-scatter.2.cloned.1.call-start
  7.2 1.0 select_reduce_fusion
  8.2 0.7 fusion.14
  8.9 1.0 scatter_custom_fusion
  9.9 7.0 %gather_fusion = bf16[128,8192]{1,0:T(8,128)(2,1)} fusion(bf16[128,8192]{1,0:T(8,128)(2,1)} %param.6, s32[1024]{0:T(1024)S(1)} %pad_clamp_fusion.1), kind=kCustom, calls=%fused_computation | custom fusion | bytes 4194816 | tf_op jit(solution)/shard_map/gather | solution.py:20
  16.9 4.4 %all_to_all.14 = bf16[64,2,8192]{2,1,0:T(2,128)(2,1)} reshape(bf16[128,8192]{1,0:T(8,128)(2,1)} %gather_fusion) | data formatting | bytes 4194304 | tf_op jit(solution)/shard_map/all_to_all | solution.py:23
  21.3 0.0 copy-start.2
  21.3 116.3 %all_to_all.21 = bf16[64,2,8192]{2,1,0:T(2,128)(2,1)S(1)} all-to-all(bf16[64,2,8192]{2,1,0:T(2,128)(2,1)} %all_to_all.14), channel_id=1, replica_groups=mesh['latent'=64,'blk'=16] {'latent'}, dimensions={0} | all-to-all | bytes 4194304 | tf_op jit(solution)/shard_map/all_to_all | solution.py:23
  137.6 0.0 copy-start.1
  137.6 1.3 copy-done.1
  138.9 0.0 copy-done.2
  138.9 3.5 subtract_convert_fusion
  142.4 0.0 copy-start.3
  142.5 4.1 %convert_element_type.34 = bf16[128,8192]{1,0:T(8,128)(2,1)} reshape(bf16[64,2,8192]{2,1,0:T(2,128)(2,1)} %subtract_convert_fusion) | data formatting | bytes 4194304 | tf_op jit(solution)/shard_map/convert_element_type | solution.py:24
  146.6 0.0 copy-done.3
  146.6 3.5 fusion.11
  150.1 4.4 %reshape.21 = f32[128,8192]{1,0:T(8,128)} reshape(bf16[64,2,8192]{2,1,0:T(2,128)(2,1)} %copy-done.1) | data formatting | bytes 6291456 | tf_op jit(solution)/shard_map/convert_element_type | solution.py:24
  154.5 0.0 copy-done
  154.5 4.1 %multiply_reduce_fusion = (f32[]{:T(128)}, bf16[128,8192]{1,0:T(8,128)(2,1)S(1)}) fusion(f32[128,8192]{1,0:T(8,128)} %reshape.21, f32[8192]{0:T(1024)S(1)} %copy-done.2, bf16[128,128]{1,0:T(8,128)(2,1)} %fusion.11, bf16[1,128,8192]{2,1,0:T(8,128)(2,1)S(1)} %copy-done), kind=kOutput, calls=%fused_computation.6 | convolution fusion | flops 273678336 | bytes 8454148 | tf_op jit(solution)/shard_map/dot_general | solution.py:28
  158.6 2.8 convolution_convert_fusion
  161.4 0.0 reduce-scatter.2.cloned.1.call-update
  161.4 10.5 %all-to-all-start.1 = ((bf16[64,2,128]{2,1,0:T(2,128)(2,1)}), bf16[64,2,128]{2,1,0:T(2,128)(2,1)S(1)}, u32[]{:S(2)}, u32[]{:S(2)}) async-start(bf16[64,2,128]{2,1,0:T(2,128)(2,1)} %bitcast.6), calls=%async_computation.1 | async-start | bytes 65536 | tf_op jit(solution)/shard_map/all_to_all | solution.py:39
  172.0 126.6 %psum.7 = f32[]{:T(128)} all-reduce(f32[]{:T(128)} %get-tuple-element.3), channel_id=1, replica_groups=mesh['latent'=64,'blk'=16] {'latent','blk'}, use_global_device_ids=true, to_apply=%region_3.4 | all-reduce | flops 1 | bytes 8 | tf_op jit(solution)/shard_map/psum | solution.py:42
  299.2 0.0 all-to-all-done.1
  299.2 1.3 gather_fusion.1
  300.5 79.6 %reduce-scatter.2.cloned.1.call-done = bf16[128,512]{1,0:T(8,128)(2,1)} async-done(((bf16[128,8192]{1,0:T(8,128)(2,1)}), bf16[128,512]{1,0:T(8,128)(2,1)}) %reduce-scatter.2.cloned.1.call-update) | async-done | bytes 131088 | tf_op jit(solution)/shard_map/reduce_scatter | solution.py:36
  380.1 1.6 multiply_bitcast_fusion
  (5 shorter events, 0.0 us)
Async XLA Ops:
  7.2 147.3 %copy-start = (bf16[1,128,8192]{2,1,0:T(8,128)(2,1)S(1)}, bf16[1,128,8192]{2,1,0:T(8,128)(2,1)}, u32[]{:S(2)}) copy-start(bf16[1,128,8192]{2,1,0:T(8,128)(2,1)} %param.10) | copy-start | bytes 6291460
  7.2 372.9 %reduce-scatter.2.cloned.1.call-start = ((), (), s32[]{:S(2)}) async-start(), calls=%async_computation.3 | async-start | bytes 2228224 | tf_op jit(solution)/shard_map/reduce_scatter | solution.py:36
  21.3 117.6 %copy-start.2 = (f32[8192]{0:T(1024)S(1)}, f32[8192]{0:T(1024)}, u32[]{:S(2)}) copy-start(f32[8192]{0:T(1024)} %param.11) | copy-start | bytes 98308
  137.6 1.3 copy-start.1
  142.4 4.1 %copy-start.3 = (f32[1,128]{1,0:T(1,128)S(1)}, f32[1,128]{1,0:T(1,128)}, u32[]{:S(2)}) copy-start(f32[1,128]{1,0:T(1,128)} %param.9) | copy-start | bytes 1540
  161.4 137.8 %all-to-all-start.1 = ((bf16[64,2,128]{2,1,0:T(2,128)(2,1)}), bf16[64,2,128]{2,1,0:T(2,128)(2,1)S(1)}, u32[]{:S(2)}, u32[]{:S(2)}) async-start(bf16[64,2,128]{2,1,0:T(2,128)(2,1)} %bitcast.6), calls=%async_computation.1 | async-start | bytes 65536 | tf_op jit(solution)/shard_map/all_to_all | solution.py:39
Sparse Core Ops, SparseCore 0:
  161.6 218.4 reduce-scatter.1
where the time goes:
time: 395 us; the launch traced here: 390 us
  blocking collectives  243 us (62%)
  waiting for transfers between devices  79.6 us (20%)
  local copies, waits for them, and re-layouts  23.5 us (6%)
  between operations  15.9 us (4%)
  starting transfers between devices  10.5 us (3%)
  matrix products  10.4 us (3%)
  other arithmetic  6.83 us (2%)
    psum x1, blocking collectives, local(): summed_loss = lax.psum(squares, ('latent', 'blk'))  127 us
    all_to_all x1, blocking collectives, local(): lax.all_to_all(outgoing, 'latent', split_axis=0, concat_axis=0, tiled=True)  116 us
    reduce_scatter x1, waiting for transfers between devices, local(): lax.psum_scatter(partial_grad.astype(jnp.bfloat16), 'blk', scatter_dimens...  79.6 us
    all_to_all x1, starting transfers between devices, local(): lax.all_to_all(codes, 'latent', split_axis=0, concat_axis=0, tiled=True)  10.5 us
    convert_element_type x2, local copies, waits for them, and re-layouts, local(): centered = (incoming.astype(jnp.float32) - dec_bias).astype(jnp.bfloat16)  8.52 us
  transfers between devices with their start and end apart: 2, of which 1 were waited for; matrix products, arithmetic and copies ran while one was open for 0% of the time, Pallas kernels for 0%

commit v1 on v0

--- a/solution.py
+++ b/solution.py
@@ -9,6 +9,7 @@
     replicas = lax.axis_size("blk")
     tok_rows = activations.shape[0]
     features = activations.shape[1]
+    width = enc_weight.shape[2]
     per_owner = tok_rows // groups
     block_of = block_ids[:, 0]
     matches = (block_of[:, None] == block_of[None, :]).astype(jnp.int32)
@@ -33,13 +34,24 @@
     partial_grad = lax.dot_general(
         codes, error_rows.astype(jnp.bfloat16), contract, preferred_element_type=jnp.float32
     )
-    summed = lax.psum_scatter(
-        partial_grad.astype(jnp.bfloat16), "blk", scatter_dimension=1, tiled=True
-    ).astype(jnp.float32)
-    returned = lax.all_to_all(codes, "latent", split_axis=0, concat_axis=0, tiled=True)
+    returned, latent_parts = lax.all_to_all(
+        (codes, jnp.full((groups, 1), squares, jnp.float32)),
+        "latent", split_axis=0, concat_axis=0, tiled=True,
+    )
+    latent_sum = jnp.sum(latent_parts)
+    chunks = (
+        partial_grad.astype(jnp.bfloat16)
+        .reshape(width, replicas, features // replicas)
+        .transpose(1, 0, 2)
+    )
+    gathered, blk_parts = lax.all_to_all(
+        (chunks, jnp.full((replicas, 1), latent_sum, jnp.float32)),
+        "blk", split_axis=0, concat_axis=0, tiled=True,
+    )
+    summed = jnp.sum(gathered.astype(jnp.float32), axis=0)
     token_codes = returned[placed]
     gradient = summed / rows_block
-    summed_loss = lax.psum(squares, ("latent", "blk"))
+    summed_loss = jnp.sum(blk_parts)
     loss_value = summed_loss / (tok_rows * groups * replicas * features)
     return (loss_value, token_codes, gradient[None])
 

time: 395 us -> 275 us (0.70); the launches traced: 390 us -> 274 us
  blocking collectives: 243 us -> 158 us
  waiting for transfers between devices: 79.6 us -> 57.1 us
  between operations: 15.9 us -> 2.51 us
    psum x1 -> x0, blocking collectives: 127 us -> none  [local(): summed_loss = lax.psum(squares, ('latent', 'blk'))]
    reduce_scatter x1 -> x0, waiting for transfers between devices: 79.6 us -> none  [local(): lax.psum_scatter(partial_grad.astype(jnp.bfloat16), 'blk', scatter_dimens...]
    all_to_all x1 -> x2, waiting for transfers between devices: 0.01 us -> 57.1 us  [the longest x1 47.6 us: local(): lax.all_to_all((chunks, jnp.full((replicas, 1), latent_sum, jnp.float32))...]
    all_to_all x0 -> x2, blocking collectives: none -> 41.3 us  [the longest x1 23.5 us: local(): lax.all_to_all((codes, jnp.full((groups, 1), squares, jnp.float32)), 'lat...]
    all_to_all x1 -> x2, starting transfers between devices: 10.5 us -> 10.5 us  [the longest x1 6.04 us: local(): lax.all_to_all((codes, jnp.full((groups, 1), squares, jnp.float32)), 'lat...]
  transfers between devices with their start and end apart: 2 -> 2, of which waited for: 1 -> 2; matrix products, arithmetic and copies ran while one was open for 0% -> 2% of each run, Pallas kernels for 0% -> 0%
where the time goes in v1:
time: 275 us; the launch traced here: 274 us
  blocking collectives  158 us (57%)
  waiting for transfers between devices  57.1 us (21%)
  local copies, waits for them, and re-layouts  26.4 us (10%)
  matrix products  11.2 us (4%)
  starting transfers between devices  10.5 us (4%)
  other arithmetic  9.13 us (3%)
    all_to_all x1, blocking collectives, local(): lax.all_to_all(outgoing, 'latent', split_axis=0, concat_axis=0, tiled=True)  116 us
    all_to_all x1, waiting for transfers between devices, local(): lax.all_to_all((chunks, jnp.full((replicas, 1), latent_sum, jnp.float32))...  47.6 us
    all_to_all x1, blocking collectives, local(): lax.all_to_all((codes, jnp.full((groups, 1), squares, jnp.float32)), 'lat...  23.5 us
    all_to_all x1, blocking collectives, local(): lax.all_to_all((chunks, jnp.full((replicas, 1), latent_sum, jnp.float32))...  17.8 us
    all_to_all x1, waiting for transfers between devices, local(): lax.all_to_all((codes, jnp.full((groups, 1), squares, jnp.float32)), 'lat...  9.44 us
    convert_element_type x2, local copies, waits for them, and re-layouts, local(): centered = (incoming.astype(jnp.float32) - dec_bias).astype(jnp.bfloat16)  8.52 us
    gather x1, local copies, waits for them, and re-layouts, local(): outgoing = activations[source_row]  6.98 us
    all_to_all x1, starting transfers between devices, local(): lax.all_to_all((codes, jnp.full((groups, 1), squares, jnp.float32)), 'lat...  6.04 us
  transfers between devices with their start and end apart: 2, of which 2 were waited for; matrix products, arithmetic and copies ran while one was open for 2% of the time, Pallas kernels for 0%

profile of v1, /device:TPU:1, one launch (start us, length us, event | category | flops | bytes accessed | tf_op | source)
XLA Modules:
  0.0 274.3 jit_solution(992572747540865462)
XLA Ops:
  0.6 0.0 copy-start
  0.7 1.0 select_reduce_fusion
  1.7 0.7 fusion.14
  2.3 1.0 scatter_custom_fusion
  3.3 7.0 %gather_fusion = bf16[128,8192]{1,0:T(8,128)(2,1)} fusion(bf16[128,8192]{1,0:T(8,128)(2,1)} %param.6, s32[1024]{0:T(1024)S(1)} %pad_clamp_fusion.1), kind=kCustom, calls=%fused_computation | custom fusion | bytes 4194816 | tf_op jit(solution)/shard_map/gather | solution.py:21
  10.3 4.4 %all_to_all.25 = bf16[64,2,8192]{2,1,0:T(2,128)(2,1)} reshape(bf16[128,8192]{1,0:T(8,128)(2,1)} %gather_fusion) | data formatting | bytes 4194304 | tf_op jit(solution)/shard_map/all_to_all | solution.py:24
  14.7 0.0 copy-start.2
  14.7 116.3 %all_to_all.38 = bf16[64,2,8192]{2,1,0:T(2,128)(2,1)S(1)} all-to-all(bf16[64,2,8192]{2,1,0:T(2,128)(2,1)} %all_to_all.25), channel_id=1, replica_groups=mesh['latent'=64,'blk'=16] {'latent'}, dimensions={0} | all-to-all | bytes 4194304 | tf_op jit(solution)/shard_map/all_to_all | solution.py:24
  131.0 0.0 copy-start.1
  131.0 1.3 copy-done.1
  132.3 0.0 copy-done.2
  132.3 3.5 %subtract_convert_fusion = bf16[64,2,8192]{2,1,0:T(2,128)(2,1)} fusion(f32[8192]{0:T(1024)S(1)} %copy-done.2, bf16[64,2,8192]{2,1,0:T(2,128)(2,1)S(1)} %all_to_all.38), kind=kLoop, calls=%fused_computation.8 | loop fusion | flops 3145728 | bytes 4227072 | tf_op jit(solution)/shard_map/convert_element_type | solution.py:25
  135.9 0.0 copy-start.3
  135.9 4.1 %convert_element_type.34 = bf16[128,8192]{1,0:T(8,128)(2,1)} reshape(bf16[64,2,8192]{2,1,0:T(2,128)(2,1)} %subtract_convert_fusion) | data formatting | bytes 4194304 | tf_op jit(solution)/shard_map/convert_element_type | solution.py:25
  140.0 0.0 copy-done.3
  140.0 3.5 %fusion.11 = bf16[128,128]{1,0:T(8,128)(2,1)} fusion(bf16[128,8192]{1,0:T(8,128)(2,1)} %convert_element_type.34, bf16[1,8192,128]{2,1,0:T(8,128)(2,1)} %param.8, f32[128]{0:T(128)S(1)} %bitcast.41), kind=kOutput, calls=%fused_computation.16 | convolution fusion | flops 268484608 | bytes 4227584 | tf_op jit(solution)/shard_map/dot_general | solution.py:26
  143.6 4.4 %reshape.40 = f32[128,8192]{1,0:T(8,128)} reshape(bf16[64,2,8192]{2,1,0:T(2,128)(2,1)} %copy-done.1) | data formatting | bytes 6291456 | tf_op jit(solution)/shard_map/convert_element_type | solution.py:25
  147.9 0.0 copy-done
  147.9 5.3 %multiply_reduce_fusion = (f32[]{:T(128)}, bf16[128,8192]{1,0:T(8,128)(2,1)}) fusion(f32[128,8192]{1,0:T(8,128)} %reshape.40, f32[8192]{0:T(1024)S(1)} %copy-done.2, bf16[128,128]{1,0:T(8,128)(2,1)} %fusion.11, bf16[1,128,8192]{2,1,0:T(8,128)(2,1)S(1)} %copy-done), kind=kOutput, calls=%fused_computation.7 | convolution fusion | flops 273678336 | bytes 8454148 | tf_op jit(solution)/shard_map/dot_general | solution.py:29
  153.3 0.7 broadcast_in_dim.20
  153.9 23.5 %all_to_all.39 = f32[64,1,1]{2,1,0:T(1,128)S(1)} all-to-all(f32[64,1,1]{2,1,0:T(1,128)S(1)} %broadcast_in_dim.20), channel_id=1, replica_groups=mesh['latent'=64,'blk'=16] {'latent'}, dimensions={0} | all-to-all | bytes 512 | tf_op jit(solution)/shard_map/all_to_all | solution.py:37
  177.5 0.7 reduce_sum.50
  178.1 0.6 broadcast_in_dim.21
  178.8 17.8 %all_to_all.40 = f32[16,1,1]{2,1,0:T(1,128)S(1)} all-to-all(f32[16,1,1]{2,1,0:T(1,128)S(1)} %broadcast_in_dim.21), channel_id=1, replica_groups=mesh['latent'=64,'blk'=16] {'blk'}, dimensions={0} | all-to-all | bytes 128 | tf_op jit(solution)/shard_map/all_to_all | solution.py:47
  196.6 6.0 %all-to-all-start.3 = ((bf16[64,2,128]{2,1,0:T(2,128)(2,1)}), bf16[64,2,128]{2,1,0:T(2,128)(2,1)S(1)}, u32[]{:S(2)}, u32[]{:S(2)}) async-start(bf16[64,2,128]{2,1,0:T(2,128)(2,1)} %bitcast.6), calls=%async_computation.3 | async-start | bytes 65536 | tf_op jit(solution)/shard_map/all_to_all | solution.py:37
  202.6 2.3 convolution_convert_fusion
  205.0 1.5 copy.18
  206.5 9.4 %all-to-all-done.3 = bf16[64,2,128]{2,1,0:T(2,128)(2,1)S(1)} async-done(((bf16[64,2,128]{2,1,0:T(2,128)(2,1)}), bf16[64,2,128]{2,1,0:T(2,128)(2,1)S(1)}, u32[]{:S(2)}, u32[]{:S(2)}) %all-to-all-start.3) | async-done | bytes 32800 | tf_op jit(solution)/shard_map/all_to_all | solution.py:37
  215.9 4.4 %all-to-all-start.4 = ((bf16[16,128,512]{2,1,0:T(8,128)(2,1)}), bf16[16,128,512]{2,1,0:T(8,128)(2,1)}, u32[]{:S(2)}, u32[]{:S(2)}) async-start(bf16[16,128,512]{2,1,0:T(8,128)(2,1)} %bitcast.37), calls=%async_computation.4 | async-start | bytes 4194304 | tf_op jit(solution)/shard_map/all_to_all | solution.py:47
  220.4 0.6 reduce_sum.51
  221.6 1.3 gather_fusion.1
  223.0 47.6 %all-to-all-done.4 = bf16[16,128,512]{2,1,0:T(8,128)(2,1)} async-done(((bf16[16,128,512]{2,1,0:T(8,128)(2,1)}), bf16[16,128,512]{2,1,0:T(8,128)(2,1)}, u32[]{:S(2)}, u32[]{:S(2)}) %all-to-all-start.4) | async-done | bytes 2097184 | tf_op jit(solution)/shard_map/all_to_all | solution.py:47
  270.6 1.9 convert_reduce_fusion
  272.5 0.7 multiply_bitcast_fusion
  (5 shorter events, 0.0 us)
Async XLA Ops:
  0.6 147.3 %copy-start = (bf16[1,128,8192]{2,1,0:T(8,128)(2,1)S(1)}, bf16[1,128,8192]{2,1,0:T(8,128)(2,1)}, u32[]{:S(2)}) copy-start(bf16[1,128,8192]{2,1,0:T(8,128)(2,1)} %param.10) | copy-start | bytes 6291460
  14.7 117.6 %copy-start.2 = (f32[8192]{0:T(1024)S(1)}, f32[8192]{0:T(1024)}, u32[]{:S(2)}) copy-start(f32[8192]{0:T(1024)} %param.11) | copy-start | bytes 98308
  131.0 1.3 copy-start.1
  135.9 4.1 %copy-start.3 = (f32[1,128]{1,0:T(1,128)S(1)}, f32[1,128]{1,0:T(1,128)}, u32[]{:S(2)}) copy-start(f32[1,128]{1,0:T(1,128)} %param.9) | copy-start | bytes 1540
  196.6 19.4 %all-to-all-start.3 = ((bf16[64,2,128]{2,1,0:T(2,128)(2,1)}), bf16[64,2,128]{2,1,0:T(2,128)(2,1)S(1)}, u32[]{:S(2)}, u32[]{:S(2)}) async-start(bf16[64,2,128]{2,1,0:T(2,128)(2,1)} %bitcast.6), calls=%async_computation.3 | async-start | bytes 65536 | tf_op jit(solution)/shard_map/all_to_all | solution.py:37
  215.9 54.6 %all-to-all-start.4 = ((bf16[16,128,512]{2,1,0:T(8,128)(2,1)}), bf16[16,128,512]{2,1,0:T(8,128)(2,1)}, u32[]{:S(2)}, u32[]{:S(2)}) async-start(bf16[16,128,512]{2,1,0:T(8,128)(2,1)} %bitcast.37), calls=%async_computation.4 | async-start | bytes 4194304 | tf_op jit(solution)/shard_map/all_to_all | solution.py:47

commit v2 on v0

v2 whole, which is shorter than its diff:
```python
import functools
import jax
import jax.numpy as jnp
from jax import lax
from jax.experimental import pallas as pl
from jax.experimental.pallas import tpu as pltpu
from jax.sharding import PartitionSpec as P

F32 = jnp.float32
BF16 = jnp.bfloat16


def _pieces_row(s, lanes):
    hi = s.astype(BF16).astype(F32)
    mid = (s - hi).astype(BF16).astype(F32)
    lo = s - hi - mid
    lane = lax.broadcasted_iota(jnp.int32, (1, lanes), 1)
    row = jnp.where(lane == 0, hi, jnp.where(lane == 1, mid, jnp.where(lane == 2, lo, 0.0)))
    return row.astype(BF16)


def _sae_kernel(x_ref, bias_ref, enc_ref, encb_ref, dec_ref, codes_ref, grad_ref,
                acc_s, codes_s, codes_t_s, sq_s, *, n_tiles, tile, chunk, replicas):
    p = pl.program_id(0)
    t = pl.program_id(1)

    @pl.when((p == 0) & (t == 0))
    def _():
        acc_s[...] = jnp.zeros_like(acc_s)
        sq_s[...] = jnp.zeros_like(sq_s)

    @pl.when(p == 0)
    def _():
        centered = (x_ref[...].astype(F32) - bias_ref[...]).astype(BF16)
        acc_s[...] += jnp.dot(centered, enc_ref[...], preferred_element_type=F32)

    @pl.when((p == 1) & (t == 0))
    def _():
        codes = jnp.maximum(acc_s[...] + encb_ref[...], 0.0)
        codes_s[...] = codes.astype(BF16)
        codes_t_s[...] = codes.T.astype(BF16)
        codes_ref[...] = codes.astype(BF16)

    @pl.when(p == 1)
    def _():
        err = (jnp.dot(codes_s[...], dec_ref[...], preferred_element_type=F32)
               + bias_ref[...] - x_ref[...].astype(F32))
        sq_s[...] += err * err
        g = jnp.dot(codes_t_s[...], err.astype(BF16), preferred_element_type=F32)
        per = tile // chunk
        for q in range(per):
            grad_ref[t * per + q, 0:g.shape[0], :] = g[:, q * chunk:(q + 1) * chunk].astype(BF16)

    @pl.when((p == 1) & (t == n_tiles - 1))
    def _():
        col = jnp.sum(sq_s[...], axis=0, keepdims=True)
        s = jnp.sum(col, axis=1, keepdims=True)
        row = _pieces_row(s, chunk)
        width = codes_s.shape[1]
        for q in range(replicas):
            grad_ref[q, width:width + 1, :] = row


def fused_step(x, bias, enc, encb, dec, *, replicas, tile=2048, interpret=False):
    rows, feat = x.shape
    width = enc.shape[1]
    n_tiles = feat // tile
    chunk = feat // replicas
    kernel = functools.partial(_sae_kernel, n_tiles=n_tiles, tile=tile, chunk=chunk, replicas=replicas)

    def enc_map(p, t):
        return (t * (1 - p) + (n_tiles - 1) * p, 0)

    def dec_map(p, t):
        return (0, t * p)

    return pl.pallas_call(
        kernel,
        grid=(2, n_tiles),
        in_specs=[
            pl.BlockSpec((rows, tile), lambda p, t: (0, t)),
            pl.BlockSpec((1, tile), lambda p, t: (0, t)),
            pl.BlockSpec((tile, width), enc_map),
            pl.BlockSpec((1, width), lambda p, t: (0, 0)),
            pl.BlockSpec((width, tile), dec_map),
        ],
        out_specs=[
            pl.BlockSpec((rows, width), lambda p, t: (0, 0)),
            pl.BlockSpec((replicas, width + 1, chunk), lambda p, t: (0, 0, 0)),
        ],
        out_shape=[
            jax.ShapeDtypeStruct((rows, width), BF16),
            jax.ShapeDtypeStruct((replicas, width + 1, chunk), BF16),
        ],
        scratch_shapes=[
            pltpu.VMEM((rows, width), F32),
            pltpu.VMEM((rows, width), BF16),
            pltpu.VMEM((width, rows), BF16),
            pltpu.VMEM((rows, tile), F32),
        ],
        compiler_params=pltpu.CompilerParams(
            dimension_semantics=("arbitrary", "arbitrary"),
            vmem_limit_bytes=48 * 1024 * 1024,
        ),
        interpret=interpret,
    )(x, bias.reshape(1, feat), enc, encb, dec)


def _split_pieces(s, lanes):
    hi = lax.reduce_precision(s, exponent_bits=8, mantissa_bits=7)
    mid = lax.reduce_precision(s - hi, exponent_bits=8, mantissa_bits=7)
    lo = s - hi - mid
    lane = jnp.arange(lanes)
    row = jnp.where(lane == 0, hi, jnp.where(lane == 1, mid, jnp.where(lane == 2, lo, 0.0)))
    return row.astype(BF16)


def local(activations, block_ids, enc_weight, enc_bias, dec_weight, dec_bias):
    groups = lax.axis_size("latent")
    replicas = lax.axis_size("blk")
    tok_rows = activations.shape[0]
    features = activations.shape[1]
    width = enc_weight.shape[2]
    per_owner = tok_rows // groups
    block_of = block_ids[:, 0]
    matches = (block_of[:, None] == block_of[None, :]).astype(jnp.int32)
    earlier = jnp.sum(jnp.tril(matches, -1), axis=1)
    placed = block_of * per_owner + earlier
    source_row = (
        jnp.zeros((tok_rows,), jnp.int32).at[placed].set(jnp.arange(tok_rows, dtype=jnp.int32))
    )
    outgoing = activations[source_row]
    rows_block = tok_rows * replicas
    incoming = lax.all_to_all(outgoing, "latent", split_axis=0, concat_axis=0, tiled=True)
    codes, grad_rows = fused_step(
        incoming, dec_bias, enc_weight[0], enc_bias, dec_weight[0], replicas=replicas
    )
    gathered = lax.all_to_all(grad_rows, "blk", split_axis=0, concat_axis=0, tiled=True)
    summed = jnp.sum(gathered[:, :width, :].astype(F32), axis=0)
    blk_sum = jnp.sum(jnp.sum(gathered[:, width, :3].astype(F32), axis=1))
    loss_row = jnp.broadcast_to(_split_pieces(blk_sum, width)[None, None, :], (groups, 1, width))
    sendback = jnp.concatenate([codes.reshape(groups, per_owner, width), loss_row], axis=1)
    returned = lax.all_to_all(sendback, "latent", split_axis=0, concat_axis=0, tiled=True)
    token_codes = returned[:, :per_owner, :].reshape(tok_rows, width)[placed]
    summed_loss = jnp.sum(jnp.sum(returned[:, per_owner, :3].astype(F32), axis=1))
    gradient = summed / rows_block
    loss_value = summed_loss / (tok_rows * groups * replicas * features)
    return (loss_value, token_codes, gradient[None])


def solution(mesh):
    placed = (
        P(("latent", "blk"), None),
        P(("latent", "blk"), None),
        P("latent", None, None),
        P("latent", None),
        P("latent", None, None),
        P(),
    )
    return jax.shard_map(
        local,
        mesh=mesh,
        in_specs=placed,
        out_specs=(P(), P(("latent", "blk"), None), P("latent", None, "blk")),
        check_vma=False,
    )
```

time: 395 us -> 243 us (0.62); the launches traced: 390 us -> 242 us
  blocking collectives: 243 us -> 116 us
  waiting for transfers between devices: 79.6 us -> 65 us
  starting transfers between devices: 10.5 us -> 21.5 us
  matrix products: 10.4 us -> 0 us
  between operations: 15.9 us -> 6.13 us
  Pallas kernels: 0 us -> 7.42 us
  local copies, waits for them, and re-layouts: 23.5 us -> 17.2 us
    psum x1 -> x0, blocking collectives: 127 us -> none  [local(): summed_loss = lax.psum(squares, ('latent', 'blk'))]
    reduce_scatter x1 -> x0, waiting for transfers between devices: 79.6 us -> none  [local(): lax.psum_scatter(partial_grad.astype(jnp.bfloat16), 'blk', scatter_dimens...]
    all_to_all x1 -> x2, waiting for transfers between devices: 0.01 us -> 65 us  [the longest x1 53.1 us: local(): lax.all_to_all(grad_rows, 'blk', split_axis=0, concat_axis=0, tiled=True)]
    all_to_all x1 -> x2, starting transfers between devices: 10.5 us -> 21.5 us  [the longest x1 12.3 us: local(): lax.all_to_all(sendback, 'latent', split_axis=0, concat_axis=0, tiled=True)]
    dot_general x3 -> x0, matrix products: 10.4 us -> none  [the longest x1 4.06 us: local(): jnp.dot(codes, dec_weight[0], preferred_element_type=jnp.float32) + dec_bias]
    convert_element_type x2 -> x0, local copies, waits for them, and re-layouts: 8.52 us -> none  [local(): centered = (incoming.astype(jnp.float32) - dec_bias).astype(jnp.bfloat16)]
    pallas_call x0 -> x1, Pallas kernels: none -> 7.42 us  [fused_step(): pl.pallas_call(kernel, grid=(2, n_tiles), in_specs=[pl.BlockSpec((rows, t...]
    all_to_all x1 -> x2, local copies, waits for them, and re-layouts: 4.4 us -> 8.52 us  [local(): lax.all_to_all(outgoing, 'latent', split_axis=0, concat_axis=0, tiled=True)]
  transfers between devices with their start and end apart: 2 -> 2, of which waited for: 1 -> 2; matrix products, arithmetic and copies ran while one was open for 0% -> 1% of each run, Pallas kernels for 0% -> 0%
where the time goes in v2:
time: 243 us; the launch traced here: 242 us
  blocking collectives  116 us (48%)
  waiting for transfers between devices  65 us (27%)
  starting transfers between devices  21.5 us (9%)
  local copies, waits for them, and re-layouts  17.2 us (7%)
  other arithmetic  8.35 us (3%)
  Pallas kernels  7.42 us (3%)
  between operations  6.13 us (3%)
    all_to_all x1, blocking collectives, local(): lax.all_to_all(outgoing, 'latent', split_axis=0, concat_axis=0, tiled=True)  116 us
    all_to_all x1, waiting for transfers between devices, local(): lax.all_to_all(grad_rows, 'blk', split_axis=0, concat_axis=0, tiled=True)  53.1 us
    all_to_all x1, starting transfers between devices, local(): lax.all_to_all(sendback, 'latent', split_axis=0, concat_axis=0, tiled=True)  12.3 us
    all_to_all x1, waiting for transfers between devices, local(): lax.all_to_all(sendback, 'latent', split_axis=0, concat_axis=0, tiled=True)  11.9 us
    all_to_all x1, starting transfers between devices, local(): lax.all_to_all(grad_rows, 'blk', split_axis=0, concat_axis=0, tiled=True)  9.14 us
    all_to_all x2, local copies, waits for them, and re-layouts, local(): lax.all_to_all(outgoing, 'latent', split_axis=0, concat_axis=0, tiled=True)  8.52 us
    pallas_call x1, Pallas kernels, fused_step(): pl.pallas_call(kernel, grid=(2, n_tiles), in_specs=[pl.BlockSpec((rows, t...  7.42 us
  transfers between devices with their start and end apart: 2, of which 2 were waited for; matrix products, arithmetic and copies ran while one was open for 1% of the time, Pallas kernels for 0%

profile of v2, /device:TPU:1, one launch (start us, length us, event | category | flops | bytes accessed | tf_op | source)
XLA Modules:
  0.0 241.9 jit_solution(1299518416635407371)
XLA Ops:
  0.6 0.0 copy-start
  0.7 1.0 select_reduce_fusion
  1.6 0.7 fusion.3
  2.3 1.0 scatter_custom_fusion
  3.3 0.0 copy-done
  3.3 3.2 %gather_fusion = bf16[128,8192]{1,0:T(8,128)(2,1)} fusion(bf16[128,8192]{1,0:T(8,128)(2,1)S(1)} %copy-done, s32[1024]{0:T(1024)S(1)} %pad_clamp_fusion.1), kind=kCustom, calls=%fused_computation | custom fusion | bytes 4194816 | tf_op jit(solution)/shard_map/gather | solution.py:132
  6.5 4.4 %all_to_all.13 = bf16[64,2,8192]{2,1,0:T(2,128)(2,1)} reshape(bf16[128,8192]{1,0:T(8,128)(2,1)} %gather_fusion) | data formatting | bytes 4194304 | tf_op jit(solution)/shard_map/all_to_all | solution.py:134
  10.9 116.3 %all_to_all.21 = bf16[64,2,8192]{2,1,0:T(2,128)(2,1)} all-to-all(bf16[64,2,8192]{2,1,0:T(2,128)(2,1)} %all_to_all.13), channel_id=1, replica_groups=mesh['latent'=64,'blk'=16] {'latent'}, dimensions={0} | all-to-all | bytes 4194304 | tf_op jit(solution)/shard_map/all_to_all | solution.py:134
  127.2 0.0 copy-start.3
  127.2 0.0 copy-start.4
  127.2 4.1 %all_to_all.15.x_ref = bf16[128,8192]{1,0:T(8,128)(2,1)} reshape(bf16[64,2,8192]{2,1,0:T(2,128)(2,1)} %all_to_all.21) | data formatting | bytes 4194304 | tf_op jit(solution)/shard_map/all_to_all | solution.py:134
  131.3 0.0 copy-done.3
  131.3 0.0 copy-done.4
  131.3 0.0 copy-start.1
  131.3 1.6 copy-done.1
  132.9 0.0 copy-start.2
  132.9 1.6 copy-done.2
  134.5 7.4 %shard_map.85 = (bf16[128,128]{1,0:T(8,128)(2,1)S(1)}, bf16[16,129,512]{2,1,0:T(8,128)(2,1)}) custom-call(bf16[128,8192]{1,0:T(8,128)(2,1)S(1)} %copy-done.1, f32[1,8192]{1,0:T(1,128)S(1)} %bitcast.15, bf16[8192,128]{1,0:T(8,128)(2,1)S(1)} %bitcast.14, f32[1,128]{1,0:T(1,128)S(1)} %copy-done.4, bf16[128,8192]{1,0:T(8,128)(2,1)} %bitcast.18), custom_call_target="tpu_custom_call" | custom-call | tf_op jit(solution)/shard_map/pallas_call | solution.py:77
  141.9 9.1 %all-to-all-start.1 = ((bf16[16,129,512]{2,1,0:T(8,128)(2,1)}), bf16[16,129,512]{2,1,0:T(8,128)(2,1)}, u32[]{:S(2)}, u32[]{:S(2)}) async-start(bf16[16,129,512]{2,1,0:T(8,128)(2,1)} %get-tuple-element.6), calls=%async_computation.1 | async-start | bytes 4456448 | tf_op jit(solution)/shard_map/all_to_all | solution.py:138
  151.1 53.1 %all-to-all-done.1 = bf16[16,129,512]{2,1,0:T(8,128)(2,1)} async-done(((bf16[16,129,512]{2,1,0:T(8,128)(2,1)}), bf16[16,129,512]{2,1,0:T(8,128)(2,1)}, u32[]{:S(2)}, u32[]{:S(2)}) %all-to-all-start.1) | async-done | bytes 2113568 | tf_op jit(solution)/shard_map/all_to_all | solution.py:138
  204.1 1.4 fusion.1
  209.1 1.3 fusion.2
  210.5 0.7 pad_maximum_fusion
  211.2 12.3 %all-to-all-start.2 = ((bf16[64,3,128]{2,1,0:T(4,128)(2,1)}), bf16[64,3,128]{2,1,0:T(4,128)(2,1)S(1)}, u32[]{:S(2)}, u32[]{:S(2)}) async-start(bf16[64,3,128]{2,1,0:T(4,128)(2,1)} %pad_maximum_fusion), calls=%async_computation.2 | async-start | bytes 131072 | tf_op jit(solution)/shard_map/all_to_all | solution.py:143
  223.5 1.9 convert_reduce_fusion
  225.4 0.7 multiply_bitcast_fusion
  226.1 11.9 %all-to-all-done.2 = bf16[64,3,128]{2,1,0:T(4,128)(2,1)S(1)} async-done(((bf16[64,3,128]{2,1,0:T(4,128)(2,1)}), bf16[64,3,128]{2,1,0:T(4,128)(2,1)S(1)}, u32[]{:S(2)}, u32[]{:S(2)}) %all-to-all-start.2) | async-done | bytes 49184 | tf_op jit(solution)/shard_map/all_to_all | solution.py:143
  238.1 1.3 gather_fusion.1
  239.4 0.7 fusion
  (7 shorter events, 0.1 us)
Async XLA Ops:
  0.6 2.7 %copy-start = (bf16[128,8192]{1,0:T(8,128)(2,1)S(1)}, bf16[128,8192]{1,0:T(8,128)(2,1)}, u32[]{:S(2)}) copy-start(bf16[128,8192]{1,0:T(8,128)(2,1)} %param.6) | copy-start | bytes 6291460
  127.2 4.1 %copy-start.3 = (f32[8192]{0:T(1024)S(1)}, f32[8192]{0:T(1024)}, u32[]{:S(2)}) copy-start(f32[8192]{0:T(1024)} %param.11) | copy-start | bytes 98308
  127.2 4.1 %copy-start.4 = (f32[1,128]{1,0:T(1,128)S(1)}, f32[1,128]{1,0:T(1,128)}, u32[]{:S(2)}) copy-start(f32[1,128]{1,0:T(1,128)} %encb_ref.1) | copy-start | bytes 1540
  131.3 1.6 copy-start.1
  132.9 1.6 copy-start.2
  141.9 62.2 %all-to-all-start.1 = ((bf16[16,129,512]{2,1,0:T(8,128)(2,1)}), bf16[16,129,512]{2,1,0:T(8,128)(2,1)}, u32[]{:S(2)}, u32[]{:S(2)}) async-start(bf16[16,129,512]{2,1,0:T(8,128)(2,1)} %get-tuple-element.6), calls=%async_computation.1 | async-start | bytes 4456448 | tf_op jit(solution)/shard_map/all_to_all | solution.py:138
  211.2 26.9 %all-to-all-start.2 = ((bf16[64,3,128]{2,1,0:T(4,128)(2,1)}), bf16[64,3,128]{2,1,0:T(4,128)(2,1)S(1)}, u32[]{:S(2)}, u32[]{:S(2)}) async-start(bf16[64,3,128]{2,1,0:T(4,128)(2,1)} %pad_maximum_fusion), calls=%async_computation.2 | async-start | bytes 131072 | tf_op jit(solution)/shard_map/all_to_all | solution.py:143

commit v3 on v2

--- a/solution.py
+++ b/solution.py
@@ -106,15 +106,6 @@
     )(x, bias.reshape(1, feat), enc, encb, dec)
 
 
-def _split_pieces(s, lanes):
-    hi = lax.reduce_precision(s, exponent_bits=8, mantissa_bits=7)
-    mid = lax.reduce_precision(s - hi, exponent_bits=8, mantissa_bits=7)
-    lo = s - hi - mid
-    lane = jnp.arange(lanes)
-    row = jnp.where(lane == 0, hi, jnp.where(lane == 1, mid, jnp.where(lane == 2, lo, 0.0)))
-    return row.astype(BF16)
-
-
 def local(activations, block_ids, enc_weight, enc_bias, dec_weight, dec_bias):
     groups = lax.axis_size("latent")
     replicas = lax.axis_size("blk")
@@ -137,12 +128,13 @@
     )
     gathered = lax.all_to_all(grad_rows, "blk", split_axis=0, concat_axis=0, tiled=True)
     summed = jnp.sum(gathered[:, :width, :].astype(F32), axis=0)
-    blk_sum = jnp.sum(jnp.sum(gathered[:, width, :3].astype(F32), axis=1))
-    loss_row = jnp.broadcast_to(_split_pieces(blk_sum, width)[None, None, :], (groups, 1, width))
+    blk_pieces = gathered[:, width, :3].reshape(1, 1, replicas * 3)
+    loss_row = jnp.pad(blk_pieces, ((0, 0), (0, 0), (0, width - replicas * 3)))
+    loss_row = jnp.broadcast_to(loss_row, (groups, 1, width))
     sendback = jnp.concatenate([codes.reshape(groups, per_owner, width), loss_row], axis=1)
     returned = lax.all_to_all(sendback, "latent", split_axis=0, concat_axis=0, tiled=True)
     token_codes = returned[:, :per_owner, :].reshape(tok_rows, width)[placed]
-    summed_loss = jnp.sum(jnp.sum(returned[:, per_owner, :3].astype(F32), axis=1))
+    summed_loss = jnp.sum(returned[:, per_owner, :].astype(F32))
     gradient = summed / rows_block
     loss_value = summed_loss / (tok_rows * groups * replicas * features)
     return (loss_value, token_codes, gradient[None])

time: 243 us -> 237 us (0.975)
  between operations: 6.13 us -> 2.51 us
  other arithmetic: 8.35 us -> 5.67 us
where the time goes in v3:
time: 237 us; the launch traced here: 236 us
  blocking collectives  116 us (49%)
  waiting for transfers between devices  65 us (27%)
  starting transfers between devices  21.5 us (9%)
  local copies, waits for them, and re-layouts  18.1 us (8%)
  Pallas kernels  7.42 us (3%)
  other arithmetic  5.67 us (2%)
  between operations  2.51 us (1%)
    all_to_all x1, blocking collectives, local(): lax.all_to_all(outgoing, 'latent', split_axis=0, concat_axis=0, tiled=True)  116 us
    all_to_all x1, waiting for transfers between devices, local(): lax.all_to_all(grad_rows, 'blk', split_axis=0, concat_axis=0, tiled=True)  53.1 us
    all_to_all x1, starting transfers between devices, local(): lax.all_to_all(sendback, 'latent', split_axis=0, concat_axis=0, tiled=True)  12.3 us
    all_to_all x1, waiting for transfers between devices, local(): lax.all_to_all(sendback, 'latent', split_axis=0, concat_axis=0, tiled=True)  11.9 us
    all_to_all x1, starting transfers between devices, local(): lax.all_to_all(grad_rows, 'blk', split_axis=0, concat_axis=0, tiled=True)  9.14 us
    all_to_all x2, local copies, waits for them, and re-layouts, local(): lax.all_to_all(outgoing, 'latent', split_axis=0, concat_axis=0, tiled=True)  8.52 us
    pallas_call x1, Pallas kernels, fused_step(): pl.pallas_call(kernel, grid=(2, n_tiles), in_specs=[pl.BlockSpec((rows, t...  7.42 us
  transfers between devices with their start and end apart: 2, of which 2 were waited for; matrix products, arithmetic and copies ran while one was open for 1% of the time, Pallas kernels for 0%

profile of v3, /device:TPU:1, one launch (start us, length us, event | category | flops | bytes accessed | tf_op | source)
XLA Modules:
  0.0 236.4 jit_solution(3814490933119023054)
XLA Ops:
  0.6 0.0 copy-start
  0.7 1.0 select_reduce_fusion
  1.6 0.7 fusion.1
  2.3 1.0 scatter_custom_fusion
  3.3 0.0 copy-done
  3.3 3.2 %gather_fusion = bf16[128,8192]{1,0:T(8,128)(2,1)} fusion(bf16[128,8192]{1,0:T(8,128)(2,1)S(1)} %copy-done, s32[1024]{0:T(1024)S(1)} %pad_clamp_fusion.1), kind=kCustom, calls=%fused_computation | custom fusion | bytes 4194816 | tf_op jit(solution)/shard_map/gather | solution.py:123
  6.5 4.4 %all_to_all.13 = bf16[64,2,8192]{2,1,0:T(2,128)(2,1)} reshape(bf16[128,8192]{1,0:T(8,128)(2,1)} %gather_fusion) | data formatting | bytes 4194304 | tf_op jit(solution)/shard_map/all_to_all | solution.py:125
  10.9 116.3 %all_to_all.21 = bf16[64,2,8192]{2,1,0:T(2,128)(2,1)} all-to-all(bf16[64,2,8192]{2,1,0:T(2,128)(2,1)} %all_to_all.13), channel_id=1, replica_groups=mesh['latent'=64,'blk'=16] {'latent'}, dimensions={0} | all-to-all | bytes 4194304 | tf_op jit(solution)/shard_map/all_to_all | solution.py:125
  127.2 0.0 copy-start.3
  127.2 0.0 copy-start.4
  127.2 4.1 %all_to_all.15.x_ref = bf16[128,8192]{1,0:T(8,128)(2,1)} reshape(bf16[64,2,8192]{2,1,0:T(2,128)(2,1)} %all_to_all.21) | data formatting | bytes 4194304 | tf_op jit(solution)/shard_map/all_to_all | solution.py:125
  131.3 0.0 copy-done.3
  131.3 0.0 copy-done.4
  131.3 0.0 copy-start.1
  131.3 1.6 copy-done.1
  132.9 0.0 copy-start.2
  132.9 1.6 copy-done.2
  134.5 7.4 %shard_map.85 = (bf16[128,128]{1,0:T(8,128)(2,1)S(1)}, bf16[16,129,512]{2,1,0:T(8,128)(2,1)}) custom-call(bf16[128,8192]{1,0:T(8,128)(2,1)S(1)} %copy-done.1, f32[1,8192]{1,0:T(1,128)S(1)} %bitcast.17, bf16[8192,128]{1,0:T(8,128)(2,1)S(1)} %bitcast.16, f32[1,128]{1,0:T(1,128)S(1)} %copy-done.4, bf16[128,8192]{1,0:T(8,128)(2,1)} %bitcast.20), custom_call_target="tpu_custom_call" | custom-call | tf_op jit(solution)/shard_map/pallas_call | solution.py:77
  141.9 9.1 %all-to-all-start.1 = ((bf16[16,129,512]{2,1,0:T(8,128)(2,1)}), bf16[16,129,512]{2,1,0:T(8,128)(2,1)}, u32[]{:S(2)}, u32[]{:S(2)}) async-start(bf16[16,129,512]{2,1,0:T(8,128)(2,1)} %get-tuple-element.6), calls=%async_computation.1 | async-start | bytes 4456448 | tf_op jit(solution)/shard_map/all_to_all | solution.py:129
  151.1 53.1 %all-to-all-done.1 = bf16[16,129,512]{2,1,0:T(8,128)(2,1)} async-done(((bf16[16,129,512]{2,1,0:T(8,128)(2,1)}), bf16[16,129,512]{2,1,0:T(8,128)(2,1)}, u32[]{:S(2)}, u32[]{:S(2)}) %all-to-all-start.1) | async-done | bytes 2113568 | tf_op jit(solution)/shard_map/all_to_all | solution.py:129
  204.1 0.8 slice_reduce_fusion
  204.9 0.1 reshape_squeeze.3
  205.1 0.7 pad_maximum_fusion
  205.8 12.3 %all-to-all-start.2 = ((bf16[64,3,128]{2,1,0:T(4,128)(2,1)}), bf16[64,3,128]{2,1,0:T(4,128)(2,1)S(1)}, u32[]{:S(2)}, u32[]{:S(2)}) async-start(bf16[64,3,128]{2,1,0:T(4,128)(2,1)} %pad_maximum_fusion), calls=%async_computation.2 | async-start | bytes 131072 | tf_op jit(solution)/shard_map/all_to_all | solution.py:135
  218.1 1.9 convert_reduce_fusion
  220.0 0.7 multiply_bitcast_fusion
  220.7 11.9 %all-to-all-done.2 = bf16[64,3,128]{2,1,0:T(4,128)(2,1)S(1)} async-done(((bf16[64,3,128]{2,1,0:T(4,128)(2,1)}), bf16[64,3,128]{2,1,0:T(4,128)(2,1)S(1)}, u32[]{:S(2)}, u32[]{:S(2)}) %all-to-all-start.2) | async-done | bytes 49184 | tf_op jit(solution)/shard_map/all_to_all | solution.py:135
  232.7 1.3 gather_fusion.1
  234.0 0.7 fusion
  (8 shorter events, 0.1 us)
Async XLA Ops:
  0.6 2.7 %copy-start = (bf16[128,8192]{1,0:T(8,128)(2,1)S(1)}, bf16[128,8192]{1,0:T(8,128)(2,1)}, u32[]{:S(2)}) copy-start(bf16[128,8192]{1,0:T(8,128)(2,1)} %param.6) | copy-start | bytes 6291460
  127.2 4.1 %copy-start.3 = (f32[8192]{0:T(1024)S(1)}, f32[8192]{0:T(1024)}, u32[]{:S(2)}) copy-start(f32[8192]{0:T(1024)} %param.11) | copy-start | bytes 98308
  127.2 4.1 %copy-start.4 = (f32[1,128]{1,0:T(1,128)S(1)}, f32[1,128]{1,0:T(1,128)}, u32[]{:S(2)}) copy-start(f32[1,128]{1,0:T(1,128)} %encb_ref.1) | copy-start | bytes 1540
  131.3 1.6 copy-start.1
  132.9 1.6 copy-start.2
  141.9 62.2 %all-to-all-start.1 = ((bf16[16,129,512]{2,1,0:T(8,128)(2,1)}), bf16[16,129,512]{2,1,0:T(8,128)(2,1)}, u32[]{:S(2)}, u32[]{:S(2)}) async-start(bf16[16,129,512]{2,1,0:T(8,128)(2,1)} %get-tuple-element.6), calls=%async_computation.1 | async-start | bytes 4456448 | tf_op jit(solution)/shard_map/all_to_all | solution.py:129
  205.8 26.9 %all-to-all-start.2 = ((bf16[64,3,128]{2,1,0:T(4,128)(2,1)}), bf16[64,3,128]{2,1,0:T(4,128)(2,1)S(1)}, u32[]{:S(2)}, u32[]{:S(2)}) async-start(bf16[64,3,128]{2,1,0:T(4,128)(2,1)} %pad_maximum_fusion), calls=%async_computation.2 | async-start | bytes 131072 | tf_op jit(solution)/shard_map/all_to_all | solution.py:135

commit v4 on v3

--- a/solution.py
+++ b/solution.py
@@ -31,22 +31,27 @@
 
     @pl.when(p == 0)
     def _():
-        centered = (x_ref[...].astype(F32) - bias_ref[...]).astype(BF16)
-        acc_s[...] += jnp.dot(centered, enc_ref[...], preferred_element_type=F32)
+        for h in range(2):
+            centered = (x_ref[:, h, :].astype(F32) - bias_ref[...]).astype(BF16)
+            acc_s[h] += jnp.dot(centered, enc_ref[...], preferred_element_type=F32)
 
     @pl.when((p == 1) & (t == 0))
     def _():
-        codes = jnp.maximum(acc_s[...] + encb_ref[...], 0.0)
-        codes_s[...] = codes.astype(BF16)
-        codes_t_s[...] = codes.T.astype(BF16)
-        codes_ref[...] = codes.astype(BF16)
+        for h in range(2):
+            codes = jnp.maximum(acc_s[h] + encb_ref[...], 0.0)
+            codes_s[h] = codes.astype(BF16)
+            codes_t_s[h] = codes.T.astype(BF16)
+            codes_ref[h] = codes.astype(BF16)
 
     @pl.when(p == 1)
     def _():
-        err = (jnp.dot(codes_s[...], dec_ref[...], preferred_element_type=F32)
-               + bias_ref[...] - x_ref[...].astype(F32))
-        sq_s[...] += err * err
-        g = jnp.dot(codes_t_s[...], err.astype(BF16), preferred_element_type=F32)
+        g = None
+        for h in range(2):
+            err = (jnp.dot(codes_s[h], dec_ref[...], preferred_element_type=F32)
+                   + bias_ref[...] - x_ref[:, h, :].astype(F32))
+            sq_s[...] += err * err
+            part = jnp.dot(codes_t_s[h], err.astype(BF16), preferred_element_type=F32)
+            g = part if g is None else g + part
         per = tile // chunk
         for q in range(per):
             grad_ref[t * per + q, 0:g.shape[0], :] = g[:, q * chunk:(q + 1) * chunk].astype(BF16)
@@ -56,13 +61,13 @@
         col = jnp.sum(sq_s[...], axis=0, keepdims=True)
         s = jnp.sum(col, axis=1, keepdims=True)
         row = _pieces_row(s, chunk)
-        width = codes_s.shape[1]
+        width = codes_s.shape[2]
         for q in range(replicas):
             grad_ref[q, width:width + 1, :] = row
 
 
 def fused_step(x, bias, enc, encb, dec, *, replicas, tile=2048, interpret=False):
-    rows, feat = x.shape
+    groups, _, feat = x.shape
     width = enc.shape[1]
     n_tiles = feat // tile
     chunk = feat // replicas
@@ -78,25 +83,25 @@
         kernel,
         grid=(2, n_tiles),
         in_specs=[
-            pl.BlockSpec((rows, tile), lambda p, t: (0, t)),
+            pl.BlockSpec((groups, 2, tile), lambda p, t: (0, 0, t)),
             pl.BlockSpec((1, tile), lambda p, t: (0, t)),
             pl.BlockSpec((tile, width), enc_map),
             pl.BlockSpec((1, width), lambda p, t: (0, 0)),
             pl.BlockSpec((width, tile), dec_map),
         ],
         out_specs=[
-            pl.BlockSpec((rows, width), lambda p, t: (0, 0)),
+            pl.BlockSpec((2, groups, width), lambda p, t: (0, 0, 0)),
             pl.BlockSpec((replicas, width + 1, chunk), lambda p, t: (0, 0, 0)),
         ],
         out_shape=[
-            jax.ShapeDtypeStruct((rows, width), BF16),
+            jax.ShapeDtypeStruct((2, groups, width), BF16),
             jax.ShapeDtypeStruct((replicas, width + 1, chunk), BF16),
         ],
         scratch_shapes=[
-            pltpu.VMEM((rows, width), F32),
-            pltpu.VMEM((rows, width), BF16),
-            pltpu.VMEM((width, rows), BF16),
-            pltpu.VMEM((rows, tile), F32),
+            pltpu.VMEM((2, groups, width), F32),
+            pltpu.VMEM((2, groups, width), BF16),
+            pltpu.VMEM((2, width, groups), BF16),
+            pltpu.VMEM((groups, tile), F32),
         ],
         compiler_params=pltpu.CompilerParams(
             dimension_semantics=("arbitrary", "arbitrary"),
@@ -120,7 +125,7 @@
     source_row = (
         jnp.zeros((tok_rows,), jnp.int32).at[placed].set(jnp.arange(tok_rows, dtype=jnp.int32))
     )
-    outgoing = activations[source_row]
+    outgoing = activations[source_row.reshape(groups, per_owner)]
     rows_block = tok_rows * replicas
     incoming = lax.all_to_all(outgoing, "latent", split_axis=0, concat_axis=0, tiled=True)
     codes, grad_rows = fused_step(
@@ -131,7 +136,7 @@
     blk_pieces = gathered[:, width, :3].reshape(1, 1, replicas * 3)
     loss_row = jnp.pad(blk_pieces, ((0, 0), (0, 0), (0, width - replicas * 3)))
     loss_row = jnp.broadcast_to(loss_row, (groups, 1, width))
-    sendback = jnp.concatenate([codes.reshape(groups, per_owner, width), loss_row], axis=1)
+    sendback = jnp.concatenate([codes.transpose(1, 0, 2), loss_row], axis=1)
     returned = lax.all_to_all(sendback, "latent", split_axis=0, concat_axis=0, tiled=True)
     token_codes = returned[:, :per_owner, :].reshape(tok_rows, width)[placed]
     summed_loss = jnp.sum(returned[:, per_owner, :].astype(F32))

time: 237 us -> 232 us (0.979)
  local copies, waits for them, and re-layouts: 18.1 us -> 11.8 us
    all_to_all x2 -> x0, local copies, waits for them, and re-layouts: 8.52 us -> none  [local(): lax.all_to_all(outgoing, 'latent', split_axis=0, concat_axis=0, tiled=True)]
    gather x1 -> x2, local copies, waits for them, and re-layouts: 3.16 us -> 7.62 us  [local(): outgoing = activations[source_row.reshape(groups, per_owner)]]
    unnamed x10 -> x8, local copies, waits for them, and re-layouts: 3.2 us -> 0.02 us
where the time goes in v4:
time: 232 us; the launch traced here: 231 us
  blocking collectives  116 us (50%)
  waiting for transfers between devices  65 us (28%)
  starting transfers between devices  21.5 us (9%)
  local copies, waits for them, and re-layouts  11.8 us (5%)
  Pallas kernels  9.3 us (4%)
  other arithmetic  5 us (2%)
  between operations  2.53 us (1%)
    all_to_all x1, blocking collectives, local(): lax.all_to_all(outgoing, 'latent', split_axis=0, concat_axis=0, tiled=True)  116 us
    all_to_all x1, waiting for transfers between devices, local(): lax.all_to_all(grad_rows, 'blk', split_axis=0, concat_axis=0, tiled=True)  53.1 us
    all_to_all x1, starting transfers between devices, local(): lax.all_to_all(sendback, 'latent', split_axis=0, concat_axis=0, tiled=True)  12.3 us
    all_to_all x1, waiting for transfers between devices, local(): lax.all_to_all(sendback, 'latent', split_axis=0, concat_axis=0, tiled=True)  11.9 us
    pallas_call x1, Pallas kernels, fused_step(): pl.pallas_call(kernel, grid=(2, n_tiles), in_specs=[pl.BlockSpec((groups,...  9.3 us
    all_to_all x1, starting transfers between devices, local(): lax.all_to_all(grad_rows, 'blk', split_axis=0, concat_axis=0, tiled=True)  9.14 us
    gather x2, local copies, waits for them, and re-layouts, local(): outgoing = activations[source_row.reshape(groups, per_owner)]  7.62 us
  transfers between devices with their start and end apart: 2, of which 2 were waited for; matrix products, arithmetic and copies ran while one was open for 1% of the time, Pallas kernels for 0%

profile of v4, /device:TPU:1, one launch (start us, length us, event | category | flops | bytes accessed | tf_op | source)
XLA Modules:
  0.0 231.4 jit_solution(13639806667310074204)
XLA Ops:
  0.6 0.0 copy-start
  0.7 1.0 select_reduce_fusion
  1.6 0.7 fusion.1
  2.3 1.0 scatter_custom_fusion
  3.3 0.1 reshape.57
  3.5 0.1 reshape.62
  3.6 0.0 copy-done
  3.6 3.2 %gather_fusion = bf16[128,8192]{1,0:T(8,128)(2,1)} fusion(bf16[128,8192]{1,0:T(8,128)(2,1)S(1)} %copy-done, s32[1024]{0:T(1024)S(1)} %pad_clamp_fusion.1), kind=kCustom, calls=%fused_computation | custom fusion | bytes 4194816 | tf_op jit(solution)/shard_map/gather | solution.py:128
  6.8 4.4 %reshape.61 = bf16[64,2,8192]{2,1,0:T(2,128)(2,1)} reshape(bf16[128,8192]{1,0:T(8,128)(2,1)} %gather_fusion) | data formatting | bytes 4194304 | tf_op jit(solution)/shard_map/gather | solution.py:128
  11.2 0.0 copy-start.1
  11.2 0.0 copy-start.2
  11.2 0.0 copy-start.3
  11.2 116.3 %all_to_all.15.x_ref = bf16[64,2,8192]{2,1,0:T(2,128)(2,1)S(1)} all-to-all(bf16[64,2,8192]{2,1,0:T(2,128)(2,1)} %reshape.61), channel_id=1, replica_groups=mesh['latent'=64,'blk'=16] {'latent'}, dimensions={0} | all-to-all | bytes 4194304 | tf_op jit(solution)/shard_map/all_to_all | solution.py:130
  127.6 0.0 copy-done.1
  127.6 0.0 copy-done.2
  127.6 0.0 copy-done.3
  127.6 9.3 %shard_map.85 = (bf16[2,64,128]{2,1,0:T(8,128)(2,1)S(1)}, bf16[16,129,512]{2,1,0:T(8,128)(2,1)}) custom-call(bf16[64,2,8192]{2,1,0:T(2,128)(2,1)S(1)} %all_to_all.15.x_ref, f32[1,8192]{1,0:T(1,128)S(1)} %bitcast.19, bf16[8192,128]{1,0:T(8,128)(2,1)S(1)} %bitcast.18, f32[1,128]{1,0:T(1,128)S(1)} %copy-done.3, bf16[128,8192]{1,0:T(8,128)(2,1)} %bitcast.22), custom_call_target="tpu_custom_call" | custom-call | tf_op jit(solution)/shard_map/pallas_call | solution.py:82
  136.9 9.1 %all-to-all-start.1 = ((bf16[16,129,512]{2,1,0:T(8,128)(2,1)}), bf16[16,129,512]{2,1,0:T(8,128)(2,1)}, u32[]{:S(2)}, u32[]{:S(2)}) async-start(bf16[16,129,512]{2,1,0:T(8,128)(2,1)} %get-tuple-element.6), calls=%async_computation.1 | async-start | bytes 4456448 | tf_op jit(solution)/shard_map/all_to_all | solution.py:134
  146.0 53.1 %all-to-all-done.1 = bf16[16,129,512]{2,1,0:T(8,128)(2,1)} async-done(((bf16[16,129,512]{2,1,0:T(8,128)(2,1)}), bf16[16,129,512]{2,1,0:T(8,128)(2,1)}, u32[]{:S(2)}, u32[]{:S(2)}) %all-to-all-start.1) | async-done | bytes 2113568 | tf_op jit(solution)/shard_map/all_to_all | solution.py:134
  199.1 0.8 slice_reduce_fusion
  199.9 0.1 reshape_squeeze.3
  200.0 0.7 copy.11
  200.7 12.3 %all-to-all-start.2 = ((bf16[64,3,128]{2,1,0:T(4,128)(2,1)}), bf16[64,3,128]{2,1,0:T(4,128)(2,1)S(1)}, u32[]{:S(2)}, u32[]{:S(2)}) async-start(bf16[64,3,128]{2,1,0:T(4,128)(2,1)} %copy.11), calls=%async_computation.2 | async-start | bytes 131072 | tf_op jit(solution)/shard_map/all_to_all | solution.py:140
  213.0 1.9 convert_reduce_fusion
  214.9 0.7 multiply_bitcast_fusion
  215.7 11.9 %all-to-all-done.2 = bf16[64,3,128]{2,1,0:T(4,128)(2,1)S(1)} async-done(((bf16[64,3,128]{2,1,0:T(4,128)(2,1)}), bf16[64,3,128]{2,1,0:T(4,128)(2,1)S(1)}, u32[]{:S(2)}, u32[]{:S(2)}) %all-to-all-start.2) | async-done | bytes 49184 | tf_op jit(solution)/shard_map/all_to_all | solution.py:140
  227.6 1.3 gather_fusion.1
  228.9 0.7 fusion
  (9 shorter events, 0.1 us)
Async XLA Ops:
  0.6 3.0 %copy-start = (bf16[128,8192]{1,0:T(8,128)(2,1)S(1)}, bf16[128,8192]{1,0:T(8,128)(2,1)}, u32[]{:S(2)}) copy-start(bf16[128,8192]{1,0:T(8,128)(2,1)} %param.6) | copy-start | bytes 6291460
  11.2 116.3 %copy-start.1 = (bf16[1,8192,128]{2,1,0:T(8,128)(2,1)S(1)}, bf16[1,8192,128]{2,1,0:T(8,128)(2,1)}, u32[]{:S(2)}) copy-start(bf16[1,8192,128]{2,1,0:T(8,128)(2,1)} %param.8) | copy-start | bytes 6291460
  11.2 116.3 %copy-start.2 = (f32[8192]{0:T(1024)S(1)}, f32[8192]{0:T(1024)}, u32[]{:S(2)}) copy-start(f32[8192]{0:T(1024)} %param.11) | copy-start | bytes 98308
  11.2 116.3 %copy-start.3 = (f32[1,128]{1,0:T(1,128)S(1)}, f32[1,128]{1,0:T(1,128)}, u32[]{:S(2)}) copy-start(f32[1,128]{1,0:T(1,128)} %encb_ref.1) | copy-start | bytes 1540
  136.9 62.2 %all-to-all-start.1 = ((bf16[16,129,512]{2,1,0:T(8,128)(2,1)}), bf16[16,129,512]{2,1,0:T(8,128)(2,1)}, u32[]{:S(2)}, u32[]{:S(2)}) async-start(bf16[16,129,512]{2,1,0:T(8,128)(2,1)} %get-tuple-element.6), calls=%async_computation.1 | async-start | bytes 4456448 | tf_op jit(solution)/shard_map/all_to_all | solution.py:134
  200.7 26.9 %all-to-all-start.2 = ((bf16[64,3,128]{2,1,0:T(4,128)(2,1)}), bf16[64,3,128]{2,1,0:T(4,128)(2,1)S(1)}, u32[]{:S(2)}, u32[]{:S(2)}) async-start(bf16[64,3,128]{2,1,0:T(4,128)(2,1)} %copy.11), calls=%async_computation.2 | async-start | bytes 131072 | tf_op jit(solution)/shard_map/all_to_all | solution.py:140

commit v5 on v4

--- a/solution.py
+++ b/solution.py
@@ -66,6 +66,30 @@
             grad_ref[q, width:width + 1, :] = row
 
 
+def _route_kernel(sel_ref, act_ref, out_ref):
+    for h in range(out_ref.shape[1]):
+        out_ref[:, h, :] = jnp.dot(
+            sel_ref[h], act_ref[...], preferred_element_type=F32).astype(out_ref.dtype)
+
+
+def route_rows(activations, placed, groups, tile=2048):
+    rows, feat = activations.shape
+    per = rows // groups
+    slot = jnp.arange(rows, dtype=jnp.int32)
+    sel = (placed[None, :] == slot[:, None]).astype(activations.dtype)
+    sel = sel.reshape(groups, per, rows).transpose(1, 0, 2)
+    return pl.pallas_call(
+        _route_kernel,
+        grid=(feat // tile,),
+        in_specs=[
+            pl.BlockSpec((per, groups, rows), lambda t: (0, 0, 0)),
+            pl.BlockSpec((rows, tile), lambda t: (0, t)),
+        ],
+        out_specs=pl.BlockSpec((groups, per, tile), lambda t: (0, 0, t)),
+        out_shape=jax.ShapeDtypeStruct((groups, per, feat), activations.dtype),
+    )(sel, activations)
+
+
 def fused_step(x, bias, enc, encb, dec, *, replicas, tile=2048, interpret=False):
     groups, _, feat = x.shape
     width = enc.shape[1]
@@ -122,10 +146,7 @@
     matches = (block_of[:, None] == block_of[None, :]).astype(jnp.int32)
     earlier = jnp.sum(jnp.tril(matches, -1), axis=1)
     placed = block_of * per_owner + earlier
-    source_row = (
-        jnp.zeros((tok_rows,), jnp.int32).at[placed].set(jnp.arange(tok_rows, dtype=jnp.int32))
-    )
-    outgoing = activations[source_row.reshape(groups, per_owner)]
+    outgoing = route_rows(activations, placed, groups)
     rows_block = tok_rows * replicas
     incoming = lax.all_to_all(outgoing, "latent", split_axis=0, concat_axis=0, tiled=True)
     codes, grad_rows = fused_step(

time: 232 us -> 228 us (0.983)
  local copies, waits for them, and re-layouts: 11.8 us -> 2.16 us
  Pallas kernels: 9.3 us -> 13.9 us
    gather x2 -> x0, local copies, waits for them, and re-layouts: 7.62 us -> none  [local(): outgoing = activations[source_row.reshape(groups, per_owner)]]
    pallas_call x0 -> x1, Pallas kernels: none -> 4.57 us  [route_rows(): pl.pallas_call(_route_kernel, grid=(feat // tile,), in_specs=[pl.BlockSpe...]
  transfers between devices with their start and end apart: 2 -> 2, of which waited for: 2 -> 2; matrix products, arithmetic and copies ran while one was open for 1% -> 0% of each run, Pallas kernels for 0% -> 0%
where the time goes in v5:
time: 228 us; the launch traced here: 227 us
  blocking collectives  116 us (51%)
  waiting for transfers between devices  66.5 us (29%)
  starting transfers between devices  21.6 us (9%)
  Pallas kernels  13.9 us (6%)
  other arithmetic  4 us (2%)
  between operations  2.5 us (1%)
    all_to_all x1, blocking collectives, local(): lax.all_to_all(outgoing, 'latent', split_axis=0, concat_axis=0, tiled=True)  116 us
    all_to_all x1, waiting for transfers between devices, local(): lax.all_to_all(grad_rows, 'blk', split_axis=0, concat_axis=0, tiled=True)  53 us
    all_to_all x1, waiting for transfers between devices, local(): lax.all_to_all(sendback, 'latent', split_axis=0, concat_axis=0, tiled=True)  13.5 us
    all_to_all x1, starting transfers between devices, local(): lax.all_to_all(sendback, 'latent', split_axis=0, concat_axis=0, tiled=True)  12.3 us
    pallas_call x1, Pallas kernels, fused_step(): pl.pallas_call(kernel, grid=(2, n_tiles), in_specs=[pl.BlockSpec((groups,...  9.33 us
    all_to_all x1, starting transfers between devices, local(): lax.all_to_all(grad_rows, 'blk', split_axis=0, concat_axis=0, tiled=True)  9.22 us
    pallas_call x1, Pallas kernels, route_rows(): pl.pallas_call(_route_kernel, grid=(feat // tile,), in_specs=[pl.BlockSpe...  4.57 us
  transfers between devices with their start and end apart: 2, of which 2 were waited for; matrix products, arithmetic and copies ran while one was open for 0% of the time, Pallas kernels for 0%

profile of v5, /device:TPU:1, one launch (start us, length us, event | category | flops | bytes accessed | tf_op | source)
XLA Modules:
  0.0 227.0 jit_solution(8415242990665623787)
XLA Ops:
  0.7 0.9 select_reduce_fusion
  1.6 0.7 multiply_add_fusion.1
  2.2 0.7 compare_convert_fusion.sel_ref
  2.9 4.6 %shard_map.85 = bf16[64,2,8192]{2,1,0:T(2,128)(2,1)} custom-call(bf16[2,64,128]{2,1,0:T(8,128)(2,1)} %compare_convert_fusion.sel_ref, bf16[128,8192]{1,0:T(8,128)(2,1)} %act_ref.1), custom_call_target="tpu_custom_call" | custom-call | tf_op jit(solution)/shard_map/pallas_call | solution.py:81
  7.5 0.0 copy-start
  7.5 0.0 copy-start.1
  7.5 0.0 copy-start.2
  7.5 116.3 %all_to_all.15.x_ref = bf16[64,2,8192]{2,1,0:T(2,128)(2,1)S(1)} all-to-all(bf16[64,2,8192]{2,1,0:T(2,128)(2,1)} %shard_map.85), channel_id=1, replica_groups=mesh['latent'=64,'blk'=16] {'latent'}, dimensions={0} | all-to-all | bytes 4194304 | tf_op jit(solution)/shard_map/all_to_all | solution.py:151
  123.8 0.0 copy-done
  123.8 0.0 copy-done.1
  123.8 0.0 copy-done.2
  123.8 9.3 %shard_map.86 = (bf16[2,64,128]{2,1,0:T(8,128)(2,1)S(1)}, bf16[16,129,512]{2,1,0:T(8,128)(2,1)}) custom-call(bf16[64,2,8192]{2,1,0:T(2,128)(2,1)S(1)} %all_to_all.15.x_ref, f32[1,8192]{1,0:T(1,128)S(1)} %bitcast.18, bf16[8192,128]{1,0:T(8,128)(2,1)S(1)} %bitcast.17, f32[1,128]{1,0:T(1,128)S(1)} %copy-done.2, bf16[128,8192]{1,0:T(8,128)(2,1)} %bitcast.21), custom_call_target="tpu_custom_call" | custom-call | tf_op jit(solution)/shard_map/pallas_call | solution.py:106
  133.2 0.0 copy-start.3
  133.2 9.2 %all-to-all-start.1 = ((bf16[16,129,512]{2,1,0:T(8,128)(2,1)}), bf16[16,129,512]{2,1,0:T(8,128)(2,1)S(1)}, u32[]{:S(2)}, u32[]{:S(2)}) async-start(bf16[16,129,512]{2,1,0:T(8,128)(2,1)} %get-tuple-element.6), calls=%async_computation.1 | async-start | bytes 4456448 | tf_op jit(solution)/shard_map/all_to_all | solution.py:155
  142.4 0.0 copy-done.3
  142.4 53.0 %all-to-all-done.1 = bf16[16,129,512]{2,1,0:T(8,128)(2,1)S(1)} async-done(((bf16[16,129,512]{2,1,0:T(8,128)(2,1)}), bf16[16,129,512]{2,1,0:T(8,128)(2,1)S(1)}, u32[]{:S(2)}, u32[]{:S(2)}) %all-to-all-start.1) | async-done | bytes 2113568 | tf_op jit(solution)/shard_map/all_to_all | solution.py:155
  195.5 0.1 reshape_squeeze.3
  195.6 0.7 copy.11
  196.3 12.3 %all-to-all-start.2 = ((bf16[64,3,128]{2,1,0:T(4,128)(2,1)}), bf16[64,3,128]{2,1,0:T(4,128)(2,1)S(1)}, u32[]{:S(2)}, u32[]{:S(2)}) async-start(bf16[64,3,128]{2,1,0:T(4,128)(2,1)} %copy.11), calls=%async_computation.2 | async-start | bytes 131072 | tf_op jit(solution)/shard_map/all_to_all | solution.py:161
  208.6 0.3 convert_reduce_fusion
  208.9 0.7 multiply_bitcast_fusion
  209.6 13.5 %all-to-all-done.2 = bf16[64,3,128]{2,1,0:T(4,128)(2,1)S(1)} async-done(((bf16[64,3,128]{2,1,0:T(4,128)(2,1)}), bf16[64,3,128]{2,1,0:T(4,128)(2,1)S(1)}, u32[]{:S(2)}, u32[]{:S(2)}) %all-to-all-start.2) | async-done | bytes 49184 | tf_op jit(solution)/shard_map/all_to_all | solution.py:161
  223.2 1.3 gather_fusion
  224.5 0.7 fusion
  (9 shorter events, 0.1 us)
Async XLA Ops:
  7.5 116.3 %copy-start = (bf16[1,8192,128]{2,1,0:T(8,128)(2,1)S(1)}, bf16[1,8192,128]{2,1,0:T(8,128)(2,1)}, u32[]{:S(2)}) copy-start(bf16[1,8192,128]{2,1,0:T(8,128)(2,1)} %param.8) | copy-start | bytes 6291460
  7.5 116.3 %copy-start.1 = (f32[8192]{0:T(1024)S(1)}, f32[8192]{0:T(1024)}, u32[]{:S(2)}) copy-start(f32[8192]{0:T(1024)} %param.11) | copy-start | bytes 98308
  7.5 116.3 %copy-start.2 = (f32[1,128]{1,0:T(1,128)S(1)}, f32[1,128]{1,0:T(1,128)}, u32[]{:S(2)}) copy-start(f32[1,128]{1,0:T(1,128)} %encb_ref.1) | copy-start | bytes 1540
  133.2 9.2 %copy-start.3 = (s32[128,1]{0,1:T(1,128)S(1)}, s32[128,1]{0,1:T(1,128)}, u32[]{:S(2)}) copy-start(s32[128,1]{0,1:T(1,128)} %param.7) | copy-start | bytes 1540
  133.2 62.2 %all-to-all-start.1 = ((bf16[16,129,512]{2,1,0:T(8,128)(2,1)}), bf16[16,129,512]{2,1,0:T(8,128)(2,1)S(1)}, u32[]{:S(2)}, u32[]{:S(2)}) async-start(bf16[16,129,512]{2,1,0:T(8,128)(2,1)} %get-tuple-element.6), calls=%async_computation.1 | async-start | bytes 4456448 | tf_op jit(solution)/shard_map/all_to_all | solution.py:155
  196.3 26.9 %all-to-all-start.2 = ((bf16[64,3,128]{2,1,0:T(4,128)(2,1)}), bf16[64,3,128]{2,1,0:T(4,128)(2,1)S(1)}, u32[]{:S(2)}, u32[]{:S(2)}) async-start(bf16[64,3,128]{2,1,0:T(4,128)(2,1)} %copy.11), calls=%async_computation.2 | async-start | bytes 131072 | tf_op jit(solution)/shard_map/all_to_all | solution.py:161

commit v6 on v5

--- a/solution.py
+++ b/solution.py
@@ -66,28 +66,35 @@
             grad_ref[q, width:width + 1, :] = row
 
 
-def _route_kernel(sel_ref, act_ref, out_ref):
-    for h in range(out_ref.shape[1]):
+def _route_kernel(col_ref, row_ref, act_ref, out_ref):
+    groups, per, _ = out_ref.shape
+    rows = col_ref.shape[0]
+    same = col_ref[...] == row_ref[...]
+    before = (lax.broadcasted_iota(jnp.int32, (rows, rows), 0)
+              < lax.broadcasted_iota(jnp.int32, (rows, rows), 1))
+    earlier = jnp.sum(jnp.where(same & before, 1.0, 0.0), axis=0, keepdims=True)
+    placed = row_ref[...].astype(F32) * per + earlier
+    slot = lax.broadcasted_iota(jnp.int32, (groups, rows), 0).astype(F32) * per
+    for h in range(per):
+        sel = jnp.where(placed == slot + h, 1.0, 0.0).astype(act_ref.dtype)
         out_ref[:, h, :] = jnp.dot(
-            sel_ref[h], act_ref[...], preferred_element_type=F32).astype(out_ref.dtype)
+            sel, act_ref[...], preferred_element_type=F32).astype(out_ref.dtype)
 
 
-def route_rows(activations, placed, groups, tile=2048):
+def route_rows(activations, block_ids, groups, tile=2048):
     rows, feat = activations.shape
     per = rows // groups
-    slot = jnp.arange(rows, dtype=jnp.int32)
-    sel = (placed[None, :] == slot[:, None]).astype(activations.dtype)
-    sel = sel.reshape(groups, per, rows).transpose(1, 0, 2)
     return pl.pallas_call(
         _route_kernel,
         grid=(feat // tile,),
         in_specs=[
-            pl.BlockSpec((per, groups, rows), lambda t: (0, 0, 0)),
+            pl.BlockSpec((rows, 1), lambda t: (0, 0)),
+            pl.BlockSpec((1, rows), lambda t: (0, 0)),
             pl.BlockSpec((rows, tile), lambda t: (0, t)),
         ],
         out_specs=pl.BlockSpec((groups, per, tile), lambda t: (0, 0, t)),
         out_shape=jax.ShapeDtypeStruct((groups, per, feat), activations.dtype),
-    )(sel, activations)
+    )(block_ids, block_ids.reshape(1, rows), activations)
 
 
 def fused_step(x, bias, enc, encb, dec, *, replicas, tile=2048, interpret=False):
@@ -146,7 +153,7 @@
     matches = (block_of[:, None] == block_of[None, :]).astype(jnp.int32)
     earlier = jnp.sum(jnp.tril(matches, -1), axis=1)
     placed = block_of * per_owner + earlier
-    outgoing = route_rows(activations, placed, groups)
+    outgoing = route_rows(activations, block_ids, groups)
     rows_block = tok_rows * replicas
     incoming = lax.all_to_all(outgoing, "latent", split_axis=0, concat_axis=0, tiled=True)
     codes, grad_rows = fused_step(

time: 228 us -> 227 us (level)
  transfers between devices with their start and end apart: 2 -> 2, of which waited for: 2 -> 2; matrix products, arithmetic and copies ran while one was open for 0% -> 1% of each run, Pallas kernels for 0% -> 0%
where the time goes in v6:
time: 227 us; the launch traced here: 226 us
  blocking collectives  116 us (51%)
  waiting for transfers between devices  66.3 us (29%)
  starting transfers between devices  21.6 us (10%)
  Pallas kernels  14.1 us (6%)
  local copies, waits for them, and re-layouts  3.55 us (2%)
  between operations  2.49 us (1%)
    all_to_all x1, blocking collectives, local(): lax.all_to_all(outgoing, 'latent', split_axis=0, concat_axis=0, tiled=True)  116 us
    all_to_all x1, waiting for transfers between devices, local(): lax.all_to_all(grad_rows, 'blk', split_axis=0, concat_axis=0, tiled=True)  52.8 us
    all_to_all x1, waiting for transfers between devices, local(): lax.all_to_all(sendback, 'latent', split_axis=0, concat_axis=0, tiled=True)  13.5 us
    all_to_all x1, starting transfers between devices, local(): lax.all_to_all(sendback, 'latent', split_axis=0, concat_axis=0, tiled=True)  12.3 us
    pallas_call x1, Pallas kernels, fused_step(): pl.pallas_call(kernel, grid=(2, n_tiles), in_specs=[pl.BlockSpec((groups,...  9.32 us
    all_to_all x1, starting transfers between devices, local(): lax.all_to_all(grad_rows, 'blk', split_axis=0, concat_axis=0, tiled=True)  9.22 us
    pallas_call x1, Pallas kernels, route_rows(): pl.pallas_call(_route_kernel, grid=(feat // tile,), in_specs=[pl.BlockSpe...  4.76 us
  transfers between devices with their start and end apart: 2, of which 2 were waited for; matrix products, arithmetic and copies ran while one was open for 1% of the time, Pallas kernels for 0%

profile of v6, /device:TPU:1, one launch (start us, length us, event | category | flops | bytes accessed | tf_op | source)
XLA Modules:
  0.0 226.2 jit_solution(7641369056545182343)
XLA Ops:
  0.6 1.4 copy.14.col_ref
  2.0 4.8 %shard_map.85 = bf16[64,2,8192]{2,1,0:T(2,128)(2,1)} custom-call(s32[128,1]{1,0:T(8,128)} %copy.14.col_ref, s32[1,128]{1,0:T(1,128)} %bitcast.22, bf16[128,8192]{1,0:T(8,128)(2,1)} %act_ref.1), custom_call_target="tpu_custom_call" | custom-call | tf_op jit(solution)/shard_map/pallas_call | solution.py:87
  6.8 0.0 copy-start
  6.8 0.0 copy-start.1
  6.8 0.0 copy-start.2
  6.8 116.3 %all_to_all.15.x_ref = bf16[64,2,8192]{2,1,0:T(2,128)(2,1)S(1)} all-to-all(bf16[64,2,8192]{2,1,0:T(2,128)(2,1)} %shard_map.85), channel_id=1, replica_groups=mesh['latent'=64,'blk'=16] {'latent'}, dimensions={0} | all-to-all | bytes 4194304 | tf_op jit(solution)/shard_map/all_to_all | solution.py:158
  123.1 0.0 copy-done
  123.1 0.0 copy-done.1
  123.1 0.0 copy-done.2
  123.1 9.3 %shard_map.86 = (bf16[2,64,128]{2,1,0:T(8,128)(2,1)S(1)}, bf16[16,129,512]{2,1,0:T(8,128)(2,1)}) custom-call(bf16[64,2,8192]{2,1,0:T(2,128)(2,1)S(1)} %all_to_all.15.x_ref, f32[1,8192]{1,0:T(1,128)S(1)} %bitcast.18, bf16[8192,128]{1,0:T(8,128)(2,1)S(1)} %bitcast.17, f32[1,128]{1,0:T(1,128)S(1)} %copy-done.2, bf16[128,8192]{1,0:T(8,128)(2,1)} %bitcast.21), custom_call_target="tpu_custom_call" | custom-call | tf_op jit(solution)/shard_map/pallas_call | solution.py:113
  132.4 0.0 copy-start.3
  132.4 9.2 %all-to-all-start.1 = ((bf16[16,129,512]{2,1,0:T(8,128)(2,1)}), bf16[16,129,512]{2,1,0:T(8,128)(2,1)S(1)}, u32[]{:S(2)}, u32[]{:S(2)}) async-start(bf16[16,129,512]{2,1,0:T(8,128)(2,1)} %get-tuple-element.6), calls=%async_computation.1 | async-start | bytes 4456448 | tf_op jit(solution)/shard_map/all_to_all | solution.py:162
  141.7 0.0 copy-done.3
  141.7 0.2 select_reduce_fusion
  141.9 52.8 %all-to-all-done.1 = bf16[16,129,512]{2,1,0:T(8,128)(2,1)S(1)} async-done(((bf16[16,129,512]{2,1,0:T(8,128)(2,1)}), bf16[16,129,512]{2,1,0:T(8,128)(2,1)S(1)}, u32[]{:S(2)}, u32[]{:S(2)}) %all-to-all-start.1) | async-done | bytes 2113568 | tf_op jit(solution)/shard_map/all_to_all | solution.py:162
  194.7 0.1 reshape_squeeze.3
  194.9 0.7 copy.15
  195.5 12.3 %all-to-all-start.2 = ((bf16[64,3,128]{2,1,0:T(4,128)(2,1)}), bf16[64,3,128]{2,1,0:T(4,128)(2,1)S(1)}, u32[]{:S(2)}, u32[]{:S(2)}) async-start(bf16[64,3,128]{2,1,0:T(4,128)(2,1)} %copy.15), calls=%async_computation.2 | async-start | bytes 131072 | tf_op jit(solution)/shard_map/all_to_all | solution.py:168
  207.9 0.3 convert_reduce_fusion
  208.2 0.7 multiply_bitcast_fusion
  208.9 13.5 %all-to-all-done.2 = bf16[64,3,128]{2,1,0:T(4,128)(2,1)S(1)} async-done(((bf16[64,3,128]{2,1,0:T(4,128)(2,1)}), bf16[64,3,128]{2,1,0:T(4,128)(2,1)S(1)}, u32[]{:S(2)}, u32[]{:S(2)}) %all-to-all-start.2) | async-done | bytes 49184 | tf_op jit(solution)/shard_map/all_to_all | solution.py:168
  222.5 1.3 gather_fusion
  223.8 0.7 fusion
  (8 shorter events, 0.1 us)
Async XLA Ops:
  6.8 116.3 %copy-start = (bf16[1,8192,128]{2,1,0:T(8,128)(2,1)S(1)}, bf16[1,8192,128]{2,1,0:T(8,128)(2,1)}, u32[]{:S(2)}) copy-start(bf16[1,8192,128]{2,1,0:T(8,128)(2,1)} %param.8) | copy-start | bytes 6291460
  6.8 116.3 %copy-start.1 = (f32[8192]{0:T(1024)S(1)}, f32[8192]{0:T(1024)}, u32[]{:S(2)}) copy-start(f32[8192]{0:T(1024)} %param.11) | copy-start | bytes 98308
  6.8 116.3 %copy-start.2 = (f32[1,128]{1,0:T(1,128)S(1)}, f32[1,128]{1,0:T(1,128)}, u32[]{:S(2)}) copy-start(f32[1,128]{1,0:T(1,128)} %encb_ref.1) | copy-start | bytes 1540
  132.4 9.2 %copy-start.3 = (s32[128,1]{0,1:T(1,128)S(1)}, s32[128,1]{0,1:T(1,128)}, u32[]{:S(2)}) copy-start(s32[128,1]{0,1:T(1,128)} %param.7) | copy-start | bytes 1540
  132.4 62.3 %all-to-all-start.1 = ((bf16[16,129,512]{2,1,0:T(8,128)(2,1)}), bf16[16,129,512]{2,1,0:T(8,128)(2,1)S(1)}, u32[]{:S(2)}, u32[]{:S(2)}) async-start(bf16[16,129,512]{2,1,0:T(8,128)(2,1)} %get-tuple-element.6), calls=%async_computation.1 | async-start | bytes 4456448 | tf_op jit(solution)/shard_map/all_to_all | solution.py:162
  195.5 26.9 %all-to-all-start.2 = ((bf16[64,3,128]{2,1,0:T(4,128)(2,1)}), bf16[64,3,128]{2,1,0:T(4,128)(2,1)S(1)}, u32[]{:S(2)}, u32[]{:S(2)}) async-start(bf16[64,3,128]{2,1,0:T(4,128)(2,1)} %copy.15), calls=%async_computation.2 | async-start | bytes 131072 | tf_op jit(solution)/shard_map/all_to_all | solution.py:168

commit v7 on v6

--- a/solution.py
+++ b/solution.py
@@ -31,27 +31,26 @@
 
     @pl.when(p == 0)
     def _():
-        for h in range(2):
-            centered = (x_ref[:, h, :].astype(F32) - bias_ref[...]).astype(BF16)
-            acc_s[h] += jnp.dot(centered, enc_ref[...], preferred_element_type=F32)
+        x = jnp.concatenate([x_ref[:, 0, :], x_ref[:, 1, :]], axis=0).astype(F32)
+        centered = (x - bias_ref[...]).astype(BF16)
+        acc_s[...] += jnp.dot(centered, enc_ref[...], preferred_element_type=F32)
 
     @pl.when((p == 1) & (t == 0))
     def _():
+        codes = jnp.maximum(acc_s[...] + encb_ref[...], 0.0)
+        codes_s[...] = codes.astype(BF16)
+        codes_t_s[...] = codes.T.astype(BF16)
+        half = codes.shape[0] // 2
         for h in range(2):
-            codes = jnp.maximum(acc_s[h] + encb_ref[...], 0.0)
-            codes_s[h] = codes.astype(BF16)
-            codes_t_s[h] = codes.T.astype(BF16)
-            codes_ref[h] = codes.astype(BF16)
+            codes_ref[h] = codes[h * half:(h + 1) * half].astype(BF16)
 
     @pl.when(p == 1)
     def _():
-        g = None
-        for h in range(2):
-            err = (jnp.dot(codes_s[h], dec_ref[...], preferred_element_type=F32)
-                   + bias_ref[...] - x_ref[:, h, :].astype(F32))
-            sq_s[...] += err * err
-            part = jnp.dot(codes_t_s[h], err.astype(BF16), preferred_element_type=F32)
-            g = part if g is None else g + part
+        x = jnp.concatenate([x_ref[:, 0, :], x_ref[:, 1, :]], axis=0).astype(F32)
+        err = (jnp.dot(codes_s[...], dec_ref[...], preferred_element_type=F32)
+               + bias_ref[...] - x)
+        sq_s[...] += err * err
+        g = jnp.dot(codes_t_s[...], err.astype(BF16), preferred_element_type=F32)
         per = tile // chunk
         for q in range(per):
             grad_ref[t * per + q, 0:g.shape[0], :] = g[:, q * chunk:(q + 1) * chunk].astype(BF16)
@@ -61,7 +60,7 @@
         col = jnp.sum(sq_s[...], axis=0, keepdims=True)
         s = jnp.sum(col, axis=1, keepdims=True)
         row = _pieces_row(s, chunk)
-        width = codes_s.shape[2]
+        width = codes_s.shape[1]
         for q in range(replicas):
             grad_ref[q, width:width + 1, :] = row
 
@@ -81,7 +80,7 @@
             sel, act_ref[...], preferred_element_type=F32).astype(out_ref.dtype)
 
 
-def route_rows(activations, block_ids, groups, tile=2048):
+def route_rows(activations, block_ids, groups, tile=4096):
     rows, feat = activations.shape
     per = rows // groups
     return pl.pallas_call(
@@ -97,7 +96,7 @@
     )(block_ids, block_ids.reshape(1, rows), activations)
 
 
-def fused_step(x, bias, enc, encb, dec, *, replicas, tile=2048, interpret=False):
+def fused_step(x, bias, enc, encb, dec, *, replicas, tile=4096, interpret=False):
     groups, _, feat = x.shape
     width = enc.shape[1]
     n_tiles = feat // tile
@@ -129,10 +128,10 @@
             jax.ShapeDtypeStruct((replicas, width + 1, chunk), BF16),
         ],
         scratch_shapes=[
-            pltpu.VMEM((2, groups, width), F32),
-            pltpu.VMEM((2, groups, width), BF16),
-            pltpu.VMEM((2, width, groups), BF16),
-            pltpu.VMEM((groups, tile), F32),
+            pltpu.VMEM((2 * groups, width), F32),
+            pltpu.VMEM((2 * groups, width), BF16),
+            pltpu.VMEM((width, 2 * groups), BF16),
+            pltpu.VMEM((2 * groups, tile), F32),
         ],
         compiler_params=pltpu.CompilerParams(
             dimension_semantics=("arbitrary", "arbitrary"),

time: 227 us -> 231 us (1.018)
  Pallas kernels: 14.1 us -> 18.3 us
    pallas_call x1, Pallas kernels: 9.32 us -> 14.3 us  [fused_step(): pl.pallas_call(kernel, grid=(2, n_tiles), in_specs=[pl.BlockSpec((groups,...]
where the time goes in v7:
time: 231 us; the launch traced here: 230 us
  blocking collectives  116 us (50%)
  waiting for transfers between devices  66.3 us (29%)
  starting transfers between devices  21.6 us (9%)
  Pallas kernels  18.3 us (8%)
  local copies, waits for them, and re-layouts  3.55 us (2%)
  between operations  2.49 us (1%)
    all_to_all x1, blocking collectives, local(): lax.all_to_all(outgoing, 'latent', split_axis=0, concat_axis=0, tiled=True)  116 us
    all_to_all x1, waiting for transfers between devices, local(): lax.all_to_all(grad_rows, 'blk', split_axis=0, concat_axis=0, tiled=True)  52.8 us
    pallas_call x1, Pallas kernels, fused_step(): pl.pallas_call(kernel, grid=(2, n_tiles), in_specs=[pl.BlockSpec((groups,...  14.3 us
    all_to_all x1, waiting for transfers between devices, local(): lax.all_to_all(sendback, 'latent', split_axis=0, concat_axis=0, tiled=True)  13.5 us
    all_to_all x1, starting transfers between devices, local(): lax.all_to_all(sendback, 'latent', split_axis=0, concat_axis=0, tiled=True)  12.3 us
    all_to_all x1, starting transfers between devices, local(): lax.all_to_all(grad_rows, 'blk', split_axis=0, concat_axis=0, tiled=True)  9.22 us
  transfers between devices with their start and end apart: 2, of which 2 were waited for; matrix products, arithmetic and copies ran while one was open for 1% of the time, Pallas kernels for 0%

profile of v7, /device:TPU:1, one launch (start us, length us, event | category | flops | bytes accessed | tf_op | source)
XLA Modules:
  0.0 230.4 jit_solution(220798678805413598)
XLA Ops:
  0.6 1.4 copy.14.col_ref
  2.0 3.9 %shard_map.85 = bf16[64,2,8192]{2,1,0:T(2,128)(2,1)} custom-call(s32[128,1]{1,0:T(8,128)} %copy.14.col_ref, s32[1,128]{1,0:T(1,128)} %bitcast.22, bf16[128,8192]{1,0:T(8,128)(2,1)} %act_ref.1), custom_call_target="tpu_custom_call" | custom-call | tf_op jit(solution)/shard_map/pallas_call | solution.py:86
  6.0 0.0 copy-start
  6.0 0.0 copy-start.1
  6.0 0.0 copy-start.2
  6.0 116.3 %all_to_all.15.x_ref = bf16[64,2,8192]{2,1,0:T(2,128)(2,1)S(1)} all-to-all(bf16[64,2,8192]{2,1,0:T(2,128)(2,1)} %shard_map.85), channel_id=1, replica_groups=mesh['latent'=64,'blk'=16] {'latent'}, dimensions={0} | all-to-all | bytes 4194304 | tf_op jit(solution)/shard_map/all_to_all | solution.py:157
  122.3 0.0 copy-done
  122.3 0.0 copy-done.1
  122.3 0.0 copy-done.2
  122.3 14.3 %shard_map.86 = (bf16[2,64,128]{2,1,0:T(8,128)(2,1)S(1)}, bf16[16,129,512]{2,1,0:T(8,128)(2,1)}) custom-call(bf16[64,2,8192]{2,1,0:T(2,128)(2,1)S(1)} %all_to_all.15.x_ref, f32[1,8192]{1,0:T(1,128)S(1)} %bitcast.18, bf16[8192,128]{1,0:T(8,128)(2,1)S(1)} %bitcast.17, f32[1,128]{1,0:T(1,128)S(1)} %copy-done.2, bf16[128,8192]{1,0:T(8,128)(2,1)} %bitcast.21), custom_call_target="tpu_custom_call" | custom-call | tf_op jit(solution)/shard_map/pallas_call | solution.py:112
  136.6 0.0 copy-start.3
  136.6 9.2 %all-to-all-start.1 = ((bf16[16,129,512]{2,1,0:T(8,128)(2,1)}), bf16[16,129,512]{2,1,0:T(8,128)(2,1)S(1)}, u32[]{:S(2)}, u32[]{:S(2)}) async-start(bf16[16,129,512]{2,1,0:T(8,128)(2,1)} %get-tuple-element.6), calls=%async_computation.1 | async-start | bytes 4456448 | tf_op jit(solution)/shard_map/all_to_all | solution.py:161
  145.9 0.0 copy-done.3
  145.9 0.2 select_reduce_fusion
  146.1 52.8 %all-to-all-done.1 = bf16[16,129,512]{2,1,0:T(8,128)(2,1)S(1)} async-done(((bf16[16,129,512]{2,1,0:T(8,128)(2,1)}), bf16[16,129,512]{2,1,0:T(8,128)(2,1)S(1)}, u32[]{:S(2)}, u32[]{:S(2)}) %all-to-all-start.1) | async-done | bytes 2113568 | tf_op jit(solution)/shard_map/all_to_all | solution.py:161
  198.9 0.1 reshape_squeeze.3
  199.1 0.7 copy.15
  199.7 12.3 %all-to-all-start.2 = ((bf16[64,3,128]{2,1,0:T(4,128)(2,1)}), bf16[64,3,128]{2,1,0:T(4,128)(2,1)S(1)}, u32[]{:S(2)}, u32[]{:S(2)}) async-start(bf16[64,3,128]{2,1,0:T(4,128)(2,1)} %copy.15), calls=%async_computation.2 | async-start | bytes 131072 | tf_op jit(solution)/shard_map/all_to_all | solution.py:167
  212.1 0.3 convert_reduce_fusion
  212.4 0.7 multiply_bitcast_fusion
  213.1 13.5 %all-to-all-done.2 = bf16[64,3,128]{2,1,0:T(4,128)(2,1)S(1)} async-done(((bf16[64,3,128]{2,1,0:T(4,128)(2,1)}), bf16[64,3,128]{2,1,0:T(4,128)(2,1)S(1)}, u32[]{:S(2)}, u32[]{:S(2)}) %all-to-all-start.2) | async-done | bytes 49184 | tf_op jit(solution)/shard_map/all_to_all | solution.py:167
  226.7 1.3 gather_fusion
  228.0 0.7 fusion
  (8 shorter events, 0.1 us)
Async XLA Ops:
  6.0 116.3 %copy-start = (bf16[1,8192,128]{2,1,0:T(8,128)(2,1)S(1)}, bf16[1,8192,128]{2,1,0:T(8,128)(2,1)}, u32[]{:S(2)}) copy-start(bf16[1,8192,128]{2,1,0:T(8,128)(2,1)} %param.8) | copy-start | bytes 6291460
  6.0 116.3 %copy-start.1 = (f32[8192]{0:T(1024)S(1)}, f32[8192]{0:T(1024)}, u32[]{:S(2)}) copy-start(f32[8192]{0:T(1024)} %param.11) | copy-start | bytes 98308
  6.0 116.3 %copy-start.2 = (f32[1,128]{1,0:T(1,128)S(1)}, f32[1,128]{1,0:T(1,128)}, u32[]{:S(2)}) copy-start(f32[1,128]{1,0:T(1,128)} %encb_ref.1) | copy-start | bytes 1540
  136.6 9.2 %copy-start.3 = (s32[128,1]{0,1:T(1,128)S(1)}, s32[128,1]{0,1:T(1,128)}, u32[]{:S(2)}) copy-start(s32[128,1]{0,1:T(1,128)} %param.7) | copy-start | bytes 1540
  136.6 62.2 %all-to-all-start.1 = ((bf16[16,129,512]{2,1,0:T(8,128)(2,1)}), bf16[16,129,512]{2,1,0:T(8,128)(2,1)S(1)}, u32[]{:S(2)}, u32[]{:S(2)}) async-start(bf16[16,129,512]{2,1,0:T(8,128)(2,1)} %get-tuple-element.6), calls=%async_computation.1 | async-start | bytes 4456448 | tf_op jit(solution)/shard_map/all_to_all | solution.py:161
  199.7 26.9 %all-to-all-start.2 = ((bf16[64,3,128]{2,1,0:T(4,128)(2,1)}), bf16[64,3,128]{2,1,0:T(4,128)(2,1)S(1)}, u32[]{:S(2)}, u32[]{:S(2)}) async-start(bf16[64,3,128]{2,1,0:T(4,128)(2,1)} %copy.15), calls=%async_computation.2 | async-start | bytes 131072 | tf_op jit(solution)/shard_map/all_to_all | solution.py:167

commit v8 on v6

--- a/solution.py
+++ b/solution.py
@@ -81,7 +81,7 @@
             sel, act_ref[...], preferred_element_type=F32).astype(out_ref.dtype)
 
 
-def route_rows(activations, block_ids, groups, tile=2048):
+def route_rows(activations, block_ids, groups, tile=4096):
     rows, feat = activations.shape
     per = rows // groups
     return pl.pallas_call(

time: 227 us -> 226 us (level)
  no operation moved by 1% of the time
where the time goes in v8:
time: 226 us; the launch traced here: 225 us
  blocking collectives  116 us (51%)
  waiting for transfers between devices  66.3 us (29%)
  starting transfers between devices  21.6 us (10%)
  Pallas kernels  13.3 us (6%)
  local copies, waits for them, and re-layouts  3.55 us (2%)
  between operations  2.49 us (1%)
    all_to_all x1, blocking collectives, local(): lax.all_to_all(outgoing, 'latent', split_axis=0, concat_axis=0, tiled=True)  116 us
    all_to_all x1, waiting for transfers between devices, local(): lax.all_to_all(grad_rows, 'blk', split_axis=0, concat_axis=0, tiled=True)  52.8 us
    all_to_all x1, waiting for transfers between devices, local(): lax.all_to_all(sendback, 'latent', split_axis=0, concat_axis=0, tiled=True)  13.5 us
    all_to_all x1, starting transfers between devices, local(): lax.all_to_all(sendback, 'latent', split_axis=0, concat_axis=0, tiled=True)  12.3 us
    pallas_call x1, Pallas kernels, fused_step(): pl.pallas_call(kernel, grid=(2, n_tiles), in_specs=[pl.BlockSpec((groups,...  9.32 us
    all_to_all x1, starting transfers between devices, local(): lax.all_to_all(grad_rows, 'blk', split_axis=0, concat_axis=0, tiled=True)  9.22 us
  transfers between devices with their start and end apart: 2, of which 2 were waited for; matrix products, arithmetic and copies ran while one was open for 1% of the time, Pallas kernels for 0%

profile of v8, /device:TPU:1, one launch (start us, length us, event | category | flops | bytes accessed | tf_op | source)
XLA Modules:
  0.0 225.4 jit_solution(10529870135892551399)
XLA Ops:
  0.6 1.4 copy.14.col_ref
  2.0 3.9 %shard_map.85 = bf16[64,2,8192]{2,1,0:T(2,128)(2,1)} custom-call(s32[128,1]{1,0:T(8,128)} %copy.14.col_ref, s32[1,128]{1,0:T(1,128)} %bitcast.22, bf16[128,8192]{1,0:T(8,128)(2,1)} %act_ref.1), custom_call_target="tpu_custom_call" | custom-call | tf_op jit(solution)/shard_map/pallas_call | solution.py:87
  6.0 0.0 copy-start
  6.0 0.0 copy-start.1
  6.0 0.0 copy-start.2
  6.0 116.3 %all_to_all.15.x_ref = bf16[64,2,8192]{2,1,0:T(2,128)(2,1)S(1)} all-to-all(bf16[64,2,8192]{2,1,0:T(2,128)(2,1)} %shard_map.85), channel_id=1, replica_groups=mesh['latent'=64,'blk'=16] {'latent'}, dimensions={0} | all-to-all | bytes 4194304 | tf_op jit(solution)/shard_map/all_to_all | solution.py:158
  122.3 0.0 copy-done
  122.3 0.0 copy-done.1
  122.3 0.0 copy-done.2
  122.3 9.3 %shard_map.86 = (bf16[2,64,128]{2,1,0:T(8,128)(2,1)S(1)}, bf16[16,129,512]{2,1,0:T(8,128)(2,1)}) custom-call(bf16[64,2,8192]{2,1,0:T(2,128)(2,1)S(1)} %all_to_all.15.x_ref, f32[1,8192]{1,0:T(1,128)S(1)} %bitcast.18, bf16[8192,128]{1,0:T(8,128)(2,1)S(1)} %bitcast.17, f32[1,128]{1,0:T(1,128)S(1)} %copy-done.2, bf16[128,8192]{1,0:T(8,128)(2,1)} %bitcast.21), custom_call_target="tpu_custom_call" | custom-call | tf_op jit(solution)/shard_map/pallas_call | solution.py:113
  131.6 0.0 copy-start.3
  131.6 9.2 %all-to-all-start.1 = ((bf16[16,129,512]{2,1,0:T(8,128)(2,1)}), bf16[16,129,512]{2,1,0:T(8,128)(2,1)S(1)}, u32[]{:S(2)}, u32[]{:S(2)}) async-start(bf16[16,129,512]{2,1,0:T(8,128)(2,1)} %get-tuple-element.6), calls=%async_computation.1 | async-start | bytes 4456448 | tf_op jit(solution)/shard_map/all_to_all | solution.py:162
  140.9 0.0 copy-done.3
  140.9 0.2 select_reduce_fusion
  141.1 52.8 %all-to-all-done.1 = bf16[16,129,512]{2,1,0:T(8,128)(2,1)S(1)} async-done(((bf16[16,129,512]{2,1,0:T(8,128)(2,1)}), bf16[16,129,512]{2,1,0:T(8,128)(2,1)S(1)}, u32[]{:S(2)}, u32[]{:S(2)}) %all-to-all-start.1) | async-done | bytes 2113568 | tf_op jit(solution)/shard_map/all_to_all | solution.py:162
  193.9 0.1 reshape_squeeze.3
  194.0 0.7 copy.15
  194.7 12.3 %all-to-all-start.2 = ((bf16[64,3,128]{2,1,0:T(4,128)(2,1)}), bf16[64,3,128]{2,1,0:T(4,128)(2,1)S(1)}, u32[]{:S(2)}, u32[]{:S(2)}) async-start(bf16[64,3,128]{2,1,0:T(4,128)(2,1)} %copy.15), calls=%async_computation.2 | async-start | bytes 131072 | tf_op jit(solution)/shard_map/all_to_all | solution.py:168
  207.1 0.3 convert_reduce_fusion
  207.4 0.7 multiply_bitcast_fusion
  208.1 13.5 %all-to-all-done.2 = bf16[64,3,128]{2,1,0:T(4,128)(2,1)S(1)} async-done(((bf16[64,3,128]{2,1,0:T(4,128)(2,1)}), bf16[64,3,128]{2,1,0:T(4,128)(2,1)S(1)}, u32[]{:S(2)}, u32[]{:S(2)}) %all-to-all-start.2) | async-done | bytes 49184 | tf_op jit(solution)/shard_map/all_to_all | solution.py:168
  221.6 1.3 gather_fusion
  223.0 0.7 fusion
  (8 shorter events, 0.1 us)
Async XLA Ops:
  6.0 116.3 %copy-start = (bf16[1,8192,128]{2,1,0:T(8,128)(2,1)S(1)}, bf16[1,8192,128]{2,1,0:T(8,128)(2,1)}, u32[]{:S(2)}) copy-start(bf16[1,8192,128]{2,1,0:T(8,128)(2,1)} %param.8) | copy-start | bytes 6291460
  6.0 116.3 %copy-start.1 = (f32[8192]{0:T(1024)S(1)}, f32[8192]{0:T(1024)}, u32[]{:S(2)}) copy-start(f32[8192]{0:T(1024)} %param.11) | copy-start | bytes 98308
  6.0 116.3 %copy-start.2 = (f32[1,128]{1,0:T(1,128)S(1)}, f32[1,128]{1,0:T(1,128)}, u32[]{:S(2)}) copy-start(f32[1,128]{1,0:T(1,128)} %encb_ref.1) | copy-start | bytes 1540
  131.6 9.2 %copy-start.3 = (s32[128,1]{0,1:T(1,128)S(1)}, s32[128,1]{0,1:T(1,128)}, u32[]{:S(2)}) copy-start(s32[128,1]{0,1:T(1,128)} %param.7) | copy-start | bytes 1540
  131.6 62.3 %all-to-all-start.1 = ((bf16[16,129,512]{2,1,0:T(8,128)(2,1)}), bf16[16,129,512]{2,1,0:T(8,128)(2,1)S(1)}, u32[]{:S(2)}, u32[]{:S(2)}) async-start(bf16[16,129,512]{2,1,0:T(8,128)(2,1)} %get-tuple-element.6), calls=%async_computation.1 | async-start | bytes 4456448 | tf_op jit(solution)/shard_map/all_to_all | solution.py:162
  194.7 26.9 %all-to-all-start.2 = ((bf16[64,3,128]{2,1,0:T(4,128)(2,1)}), bf16[64,3,128]{2,1,0:T(4,128)(2,1)S(1)}, u32[]{:S(2)}, u32[]{:S(2)}) async-start(bf16[64,3,128]{2,1,0:T(4,128)(2,1)} %copy.15), calls=%async_computation.2 | async-start | bytes 131072 | tf_op jit(solution)/shard_map/all_to_all | solution.py:168

commit v9 on v8

--- a/solution.py
+++ b/solution.py
@@ -23,6 +23,7 @@
                 acc_s, codes_s, codes_t_s, sq_s, *, n_tiles, tile, chunk, replicas):
     p = pl.program_id(0)
     t = pl.program_id(1)
+    cols = pl.ds(pl.multiple_of(t * tile, tile), tile)
 
     @pl.when((p == 0) & (t == 0))
     def _():
@@ -32,7 +33,7 @@
     @pl.when(p == 0)
     def _():
         for h in range(2):
-            centered = (x_ref[:, h, :].astype(F32) - bias_ref[...]).astype(BF16)
+            centered = (x_ref[:, h, cols].astype(F32) - bias_ref[...]).astype(BF16)
             acc_s[h] += jnp.dot(centered, enc_ref[...], preferred_element_type=F32)
 
     @pl.when((p == 1) & (t == 0))
@@ -48,7 +49,7 @@
         g = None
         for h in range(2):
             err = (jnp.dot(codes_s[h], dec_ref[...], preferred_element_type=F32)
-                   + bias_ref[...] - x_ref[:, h, :].astype(F32))
+                   + bias_ref[...] - x_ref[:, h, cols].astype(F32))
             sq_s[...] += err * err
             part = jnp.dot(codes_t_s[h], err.astype(BF16), preferred_element_type=F32)
             g = part if g is None else g + part
@@ -114,7 +115,7 @@
         kernel,
         grid=(2, n_tiles),
         in_specs=[
-            pl.BlockSpec((groups, 2, tile), lambda p, t: (0, 0, t)),
+            pl.BlockSpec(memory_space=pltpu.VMEM),
             pl.BlockSpec((1, tile), lambda p, t: (0, t)),
             pl.BlockSpec((tile, width), enc_map),
             pl.BlockSpec((1, width), lambda p, t: (0, 0)),

time: 226 us -> 226 us (level)
  no operation moved by 1% of the time
where the time goes in v9:
time: 226 us; the launch traced here: 225 us
  blocking collectives  116 us (51%)
  waiting for transfers between devices  66.3 us (29%)
  starting transfers between devices  21.6 us (10%)
  Pallas kernels  13 us (6%)
  local copies, waits for them, and re-layouts  3.55 us (2%)
  between operations  2.49 us (1%)
    all_to_all x1, blocking collectives, local(): lax.all_to_all(outgoing, 'latent', split_axis=0, concat_axis=0, tiled=True)  116 us
    all_to_all x1, waiting for transfers between devices, local(): lax.all_to_all(grad_rows, 'blk', split_axis=0, concat_axis=0, tiled=True)  52.8 us
    all_to_all x1, waiting for transfers between devices, local(): lax.all_to_all(sendback, 'latent', split_axis=0, concat_axis=0, tiled=True)  13.5 us
    all_to_all x1, starting transfers between devices, local(): lax.all_to_all(sendback, 'latent', split_axis=0, concat_axis=0, tiled=True)  12.3 us
    all_to_all x1, starting transfers between devices, local(): lax.all_to_all(grad_rows, 'blk', split_axis=0, concat_axis=0, tiled=True)  9.22 us
    pallas_call x1, Pallas kernels, fused_step(): pl.pallas_call(kernel, grid=(2, n_tiles), in_specs=[pl.BlockSpec(memory_s...  9.11 us
  transfers between devices with their start and end apart: 2, of which 2 were waited for; matrix products, arithmetic and copies ran while one was open for 1% of the time, Pallas kernels for 0%

profile of v9, /device:TPU:1, one launch (start us, length us, event | category | flops | bytes accessed | tf_op | source)
XLA Modules:
  0.0 225.2 jit_solution(16662332442611343906)
XLA Ops:
  0.6 1.4 copy.14.col_ref
  2.0 3.9 %shard_map.85 = bf16[64,2,8192]{2,1,0:T(2,128)(2,1)} custom-call(s32[128,1]{1,0:T(8,128)} %copy.14.col_ref, s32[1,128]{1,0:T(1,128)} %bitcast.22, bf16[128,8192]{1,0:T(8,128)(2,1)} %act_ref.1), custom_call_target="tpu_custom_call" | custom-call | tf_op jit(solution)/shard_map/pallas_call | solution.py:88
  6.0 0.0 copy-start
  6.0 0.0 copy-start.1
  6.0 0.0 copy-start.2
  6.0 116.3 %all_to_all.15.x_ref = bf16[64,2,8192]{2,1,0:T(2,128)(2,1)S(1)} all-to-all(bf16[64,2,8192]{2,1,0:T(2,128)(2,1)} %shard_map.85), channel_id=1, replica_groups=mesh['latent'=64,'blk'=16] {'latent'}, dimensions={0} | all-to-all | bytes 4194304 | tf_op jit(solution)/shard_map/all_to_all | solution.py:159
  122.3 0.0 copy-done
  122.3 0.0 copy-done.1
  122.3 0.0 copy-done.2
  122.3 9.1 %shard_map.86 = (bf16[2,64,128]{2,1,0:T(8,128)(2,1)S(1)}, bf16[16,129,512]{2,1,0:T(8,128)(2,1)}) custom-call(bf16[64,2,8192]{2,1,0:T(2,128)(2,1)S(1)} %all_to_all.15.x_ref, f32[1,8192]{1,0:T(1,128)S(1)} %bitcast.18, bf16[8192,128]{1,0:T(8,128)(2,1)S(1)} %bitcast.17, f32[1,128]{1,0:T(1,128)S(1)} %copy-done.2, bf16[128,8192]{1,0:T(8,128)(2,1)} %bitcast.21), custom_call_target="tpu_custom_call" | custom-call | tf_op jit(solution)/shard_map/pallas_call | solution.py:114
  131.4 0.0 copy-start.3
  131.4 9.2 %all-to-all-start.1 = ((bf16[16,129,512]{2,1,0:T(8,128)(2,1)}), bf16[16,129,512]{2,1,0:T(8,128)(2,1)S(1)}, u32[]{:S(2)}, u32[]{:S(2)}) async-start(bf16[16,129,512]{2,1,0:T(8,128)(2,1)} %get-tuple-element.6), calls=%async_computation.1 | async-start | bytes 4456448 | tf_op jit(solution)/shard_map/all_to_all | solution.py:163
  140.6 0.0 copy-done.3
  140.7 0.2 select_reduce_fusion
  140.9 52.8 %all-to-all-done.1 = bf16[16,129,512]{2,1,0:T(8,128)(2,1)S(1)} async-done(((bf16[16,129,512]{2,1,0:T(8,128)(2,1)}), bf16[16,129,512]{2,1,0:T(8,128)(2,1)S(1)}, u32[]{:S(2)}, u32[]{:S(2)}) %all-to-all-start.1) | async-done | bytes 2113568 | tf_op jit(solution)/shard_map/all_to_all | solution.py:163
  193.7 0.1 reshape_squeeze.3
  193.8 0.7 copy.15
  194.5 12.3 %all-to-all-start.2 = ((bf16[64,3,128]{2,1,0:T(4,128)(2,1)}), bf16[64,3,128]{2,1,0:T(4,128)(2,1)S(1)}, u32[]{:S(2)}, u32[]{:S(2)}) async-start(bf16[64,3,128]{2,1,0:T(4,128)(2,1)} %copy.15), calls=%async_computation.2 | async-start | bytes 131072 | tf_op jit(solution)/shard_map/all_to_all | solution.py:169
  206.8 0.3 convert_reduce_fusion
  207.2 0.7 multiply_bitcast_fusion
  207.9 13.5 %all-to-all-done.2 = bf16[64,3,128]{2,1,0:T(4,128)(2,1)S(1)} async-done(((bf16[64,3,128]{2,1,0:T(4,128)(2,1)}), bf16[64,3,128]{2,1,0:T(4,128)(2,1)S(1)}, u32[]{:S(2)}, u32[]{:S(2)}) %all-to-all-start.2) | async-done | bytes 49184 | tf_op jit(solution)/shard_map/all_to_all | solution.py:169
  221.4 1.3 gather_fusion
  222.8 0.7 fusion
  (8 shorter events, 0.1 us)
Async XLA Ops:
  6.0 116.3 %copy-start = (bf16[1,8192,128]{2,1,0:T(8,128)(2,1)S(1)}, bf16[1,8192,128]{2,1,0:T(8,128)(2,1)}, u32[]{:S(2)}) copy-start(bf16[1,8192,128]{2,1,0:T(8,128)(2,1)} %param.8) | copy-start | bytes 6291460
  6.0 116.3 %copy-start.1 = (f32[8192]{0:T(1024)S(1)}, f32[8192]{0:T(1024)}, u32[]{:S(2)}) copy-start(f32[8192]{0:T(1024)} %param.11) | copy-start | bytes 98308
  6.0 116.3 %copy-start.2 = (f32[1,128]{1,0:T(1,128)S(1)}, f32[1,128]{1,0:T(1,128)}, u32[]{:S(2)}) copy-start(f32[1,128]{1,0:T(1,128)} %encb_ref.1) | copy-start | bytes 1540
  131.4 9.2 %copy-start.3 = (s32[128,1]{0,1:T(1,128)S(1)}, s32[128,1]{0,1:T(1,128)}, u32[]{:S(2)}) copy-start(s32[128,1]{0,1:T(1,128)} %param.7) | copy-start | bytes 1540
  131.4 62.2 %all-to-all-start.1 = ((bf16[16,129,512]{2,1,0:T(8,128)(2,1)}), bf16[16,129,512]{2,1,0:T(8,128)(2,1)S(1)}, u32[]{:S(2)}, u32[]{:S(2)}) async-start(bf16[16,129,512]{2,1,0:T(8,128)(2,1)} %get-tuple-element.6), calls=%async_computation.1 | async-start | bytes 4456448 | tf_op jit(solution)/shard_map/all_to_all | solution.py:163
  194.5 26.9 %all-to-all-start.2 = ((bf16[64,3,128]{2,1,0:T(4,128)(2,1)}), bf16[64,3,128]{2,1,0:T(4,128)(2,1)S(1)}, u32[]{:S(2)}, u32[]{:S(2)}) async-start(bf16[64,3,128]{2,1,0:T(4,128)(2,1)} %copy.15), calls=%async_computation.2 | async-start | bytes 131072 | tf_op jit(solution)/shard_map/all_to_all | solution.py:169

commit v10 on v9

--- a/solution.py
+++ b/solution.py
@@ -98,7 +98,7 @@
     )(block_ids, block_ids.reshape(1, rows), activations)
 
 
-def fused_step(x, bias, enc, encb, dec, *, replicas, tile=2048, interpret=False):
+def fused_step(x, bias, enc, encb, dec, *, replicas, tile=4096, interpret=False):
     groups, _, feat = x.shape
     width = enc.shape[1]
     n_tiles = feat // tile

time: 226 us -> 225 us (level)
  no operation moved by 1% of the time
where the time goes in v10:
time: 225 us
  blocking collectives  116 us (52%)
  waiting for transfers between devices  66.3 us (29%)
  starting transfers between devices  21.6 us (10%)
  Pallas kernels  12.6 us (6%)
  local copies, waits for them, and re-layouts  3.55 us (2%)
  between operations  2.49 us (1%)
    all_to_all x1, blocking collectives, local(): lax.all_to_all(outgoing, 'latent', split_axis=0, concat_axis=0, tiled=True)  116 us
    all_to_all x1, waiting for transfers between devices, local(): lax.all_to_all(grad_rows, 'blk', split_axis=0, concat_axis=0, tiled=True)  52.8 us
    all_to_all x1, waiting for transfers between devices, local(): lax.all_to_all(sendback, 'latent', split_axis=0, concat_axis=0, tiled=True)  13.5 us
    all_to_all x1, starting transfers between devices, local(): lax.all_to_all(sendback, 'latent', split_axis=0, concat_axis=0, tiled=True)  12.3 us
    all_to_all x1, starting transfers between devices, local(): lax.all_to_all(grad_rows, 'blk', split_axis=0, concat_axis=0, tiled=True)  9.22 us
    pallas_call x1, Pallas kernels, fused_step(): pl.pallas_call(kernel, grid=(2, n_tiles), in_specs=[pl.BlockSpec(memory_s...  8.63 us
  transfers between devices with their start and end apart: 2, of which 2 were waited for; matrix products, arithmetic and copies ran while one was open for 1% of the time, Pallas kernels for 0%

profile of v10, /device:TPU:1, one launch (start us, length us, event | category | flops | bytes accessed | tf_op | source)
XLA Modules:
  0.0 224.7 jit_solution(9773180584247094327)
XLA Ops:
  0.6 1.4 copy.14.col_ref
  2.0 3.9 %shard_map.85 = bf16[64,2,8192]{2,1,0:T(2,128)(2,1)} custom-call(s32[128,1]{1,0:T(8,128)} %copy.14.col_ref, s32[1,128]{1,0:T(1,128)} %bitcast.22, bf16[128,8192]{1,0:T(8,128)(2,1)} %act_ref.1), custom_call_target="tpu_custom_call" | custom-call | tf_op jit(solution)/shard_map/pallas_call | solution.py:88
  6.0 0.0 copy-start
  6.0 0.0 copy-start.1
  6.0 0.0 copy-start.2
  6.0 116.3 %all_to_all.15.x_ref = bf16[64,2,8192]{2,1,0:T(2,128)(2,1)S(1)} all-to-all(bf16[64,2,8192]{2,1,0:T(2,128)(2,1)} %shard_map.85), channel_id=1, replica_groups=mesh['latent'=64,'blk'=16] {'latent'}, dimensions={0} | all-to-all | bytes 4194304 | tf_op jit(solution)/shard_map/all_to_all | solution.py:159
  122.3 0.0 copy-done
  122.3 0.0 copy-done.1
  122.3 0.0 copy-done.2
  122.3 8.6 %shard_map.86 = (bf16[2,64,128]{2,1,0:T(8,128)(2,1)S(1)}, bf16[16,129,512]{2,1,0:T(8,128)(2,1)}) custom-call(bf16[64,2,8192]{2,1,0:T(2,128)(2,1)S(1)} %all_to_all.15.x_ref, f32[1,8192]{1,0:T(1,128)S(1)} %bitcast.18, bf16[8192,128]{1,0:T(8,128)(2,1)S(1)} %bitcast.17, f32[1,128]{1,0:T(1,128)S(1)} %copy-done.2, bf16[128,8192]{1,0:T(8,128)(2,1)} %bitcast.21), custom_call_target="tpu_custom_call" | custom-call | tf_op jit(solution)/shard_map/pallas_call | solution.py:114
  130.9 0.0 copy-start.3
  130.9 9.2 %all-to-all-start.1 = ((bf16[16,129,512]{2,1,0:T(8,128)(2,1)}), bf16[16,129,512]{2,1,0:T(8,128)(2,1)S(1)}, u32[]{:S(2)}, u32[]{:S(2)}) async-start(bf16[16,129,512]{2,1,0:T(8,128)(2,1)} %get-tuple-element.6), calls=%async_computation.1 | async-start | bytes 4456448 | tf_op jit(solution)/shard_map/all_to_all | solution.py:163
  140.2 0.0 copy-done.3
  140.2 0.2 select_reduce_fusion
  140.4 52.8 %all-to-all-done.1 = bf16[16,129,512]{2,1,0:T(8,128)(2,1)S(1)} async-done(((bf16[16,129,512]{2,1,0:T(8,128)(2,1)}), bf16[16,129,512]{2,1,0:T(8,128)(2,1)S(1)}, u32[]{:S(2)}, u32[]{:S(2)}) %all-to-all-start.1) | async-done | bytes 2113568 | tf_op jit(solution)/shard_map/all_to_all | solution.py:163
  193.2 0.1 reshape_squeeze.3
  193.3 0.7 copy.15
  194.0 12.3 %all-to-all-start.2 = ((bf16[64,3,128]{2,1,0:T(4,128)(2,1)}), bf16[64,3,128]{2,1,0:T(4,128)(2,1)S(1)}, u32[]{:S(2)}, u32[]{:S(2)}) async-start(bf16[64,3,128]{2,1,0:T(4,128)(2,1)} %copy.15), calls=%async_computation.2 | async-start | bytes 131072 | tf_op jit(solution)/shard_map/all_to_all | solution.py:169
  206.4 0.3 convert_reduce_fusion
  206.7 0.7 multiply_bitcast_fusion
  207.4 13.5 %all-to-all-done.2 = bf16[64,3,128]{2,1,0:T(4,128)(2,1)S(1)} async-done(((bf16[64,3,128]{2,1,0:T(4,128)(2,1)}), bf16[64,3,128]{2,1,0:T(4,128)(2,1)S(1)}, u32[]{:S(2)}, u32[]{:S(2)}) %all-to-all-start.2) | async-done | bytes 49184 | tf_op jit(solution)/shard_map/all_to_all | solution.py:169
  221.0 1.3 gather_fusion
  222.3 0.7 fusion
  (8 shorter events, 0.1 us)
Async XLA Ops:
  6.0 116.3 %copy-start = (bf16[1,8192,128]{2,1,0:T(8,128)(2,1)S(1)}, bf16[1,8192,128]{2,1,0:T(8,128)(2,1)}, u32[]{:S(2)}) copy-start(bf16[1,8192,128]{2,1,0:T(8,128)(2,1)} %param.8) | copy-start | bytes 6291460
  6.0 116.3 %copy-start.1 = (f32[8192]{0:T(1024)S(1)}, f32[8192]{0:T(1024)}, u32[]{:S(2)}) copy-start(f32[8192]{0:T(1024)} %param.11) | copy-start | bytes 98308
  6.0 116.3 %copy-start.2 = (f32[1,128]{1,0:T(1,128)S(1)}, f32[1,128]{1,0:T(1,128)}, u32[]{:S(2)}) copy-start(f32[1,128]{1,0:T(1,128)} %encb_ref.1) | copy-start | bytes 1540
  130.9 9.2 %copy-start.3 = (s32[128,1]{0,1:T(1,128)S(1)}, s32[128,1]{0,1:T(1,128)}, u32[]{:S(2)}) copy-start(s32[128,1]{0,1:T(1,128)} %param.7) | copy-start | bytes 1540
  130.9 62.2 %all-to-all-start.1 = ((bf16[16,129,512]{2,1,0:T(8,128)(2,1)}), bf16[16,129,512]{2,1,0:T(8,128)(2,1)S(1)}, u32[]{:S(2)}, u32[]{:S(2)}) async-start(bf16[16,129,512]{2,1,0:T(8,128)(2,1)} %get-tuple-element.6), calls=%async_computation.1 | async-start | bytes 4456448 | tf_op jit(solution)/shard_map/all_to_all | solution.py:163
  194.0 26.9 %all-to-all-start.2 = ((bf16[64,3,128]{2,1,0:T(4,128)(2,1)}), bf16[64,3,128]{2,1,0:T(4,128)(2,1)S(1)}, u32[]{:S(2)}, u32[]{:S(2)}) async-start(bf16[64,3,128]{2,1,0:T(4,128)(2,1)} %copy.15), calls=%async_computation.2 | async-start | bytes 131072 | tf_op jit(solution)/shard_map/all_to_all | solution.py:169
